TPU v7x, 128 devices: a whole 4x4x4 slice. The times are simulated.
128 devices in a mesh: wa: 16 (over x, z), ha: 8 (over y, core).
Axes of the slice: x: 4, y: 4, z: 4, core: 2. Of those that a mesh axis runs over, the one named last changes fastest.
Arguments:
- tokens: bfloat16 [512, 16384], P('ha', 'wa'), may hold values from -100 to 100, as said below
- norm_gain: float32 [16384], P('wa'), may hold values from 0.5 to 1.5
- gate_weight: bfloat16 [16384, 26624], P('wa', 'ha'), may hold values from -0.046875 to 0.046875
- up_weight: bfloat16 [16384, 26624], P('wa', 'ha'), may hold values from -0.046875 to 0.046875
- down_weight: bfloat16 [26624, 16384], P('ha', 'wa'), may hold values from -0.0390625 to 0.0390625
Outputs:
- mixed: bfloat16 [512, 16384], P('ha', 'wa')
Inputs may be any that keep to these rules, and one draw needn't show every extreme that they name: `tokens`: real-valued activations.
All inputs are finite; a program needn't handle non-finite values.
Results may differ from a plain program's by a relative error of at most 0.0064.
Values may be sent and summed in bfloat16 or wider, within the bound.
A program may use at most 128 MiB of HBM per device.

v0:
```python
import jax
import jax.numpy as jnp
from jax import lax
from jax.sharding import PartitionSpec as P


def apply_norm(own_values, squares, norm_gain):
    model_width = own_values.shape[1] * lax.axis_size("wa")
    mean_square = squares[:, None] / model_width
    return (own_values * lax.rsqrt(mean_square + 1e-05) * norm_gain[None, :]).astype(jnp.bfloat16)


def activate(summed, hidden_width):
    gate = summed[:, :hidden_width]
    up = summed[:, hidden_width:]
    return (jax.nn.silu(gate) * up).astype(jnp.bfloat16)


def body(tokens, norm_gain, gate_weight, up_weight, down_weight):
    gathered = lax.all_gather(tokens, "ha", axis=0, tiled=True)
    own_values = gathered.astype(jnp.float32)
    squares = lax.psum(jnp.sum(own_values * own_values, axis=1), "wa")
    normed = apply_norm(own_values, squares, norm_gain)
    hidden_width = gate_weight.shape[1]
    gate_part = jnp.dot(normed, gate_weight, preferred_element_type=jnp.float32)
    up_part = jnp.dot(normed, up_weight, preferred_element_type=jnp.float32)
    summed = lax.psum_scatter(
        jnp.concatenate([gate_part, up_part], axis=1), "wa", scatter_dimension=0, tiled=True
    )
    hidden = activate(summed, hidden_width)
    partial_out = jnp.dot(
        lax.all_gather(hidden, "wa", axis=0, tiled=True),
        down_weight,
        preferred_element_type=jnp.float32,
    )
    mixed_out = lax.psum_scatter(partial_out, "ha", scatter_dimension=0, tiled=True)
    return mixed_out.astype(jnp.bfloat16)


def solution(mesh):
    placed = (P("ha", "wa"), P("wa"), P("wa", "ha"), P("wa", "ha"), P("ha", "wa"))
    return jax.shard_map(body, mesh=mesh, in_specs=placed, out_specs=P("ha", "wa"), check_vma=False)
```

profile of v0, /device:TPU:1, one launch (start us, length us, event | category | flops | bytes accessed | tf_op | source)
XLA Modules:
  0.0 283.5 jit_solution(6064925622431984980)
XLA Ops:
  6.5 0.0 all-gather.3.cloned.1.call-start
  6.5 0.7 all-gather.3.cloned.1.call-update
  7.3 0.0 reduce-scatter.3.cloned.1.call-start
  7.3 28.8 %all-gather.3.cloned.1.call-done = bf16[512,1024]{1,0:T(8,128)(2,1)} async-done(((bf16[64,1024]{1,0:T(8,128)(2,1)}), bf16[512,1024]{1,0:T(8,128)(2,1)}) %all-gather.3.cloned.1.call-update) | async-done | bytes 1048592 | tf_op jit(solution)/shard_map/all_gather | solution.py:20
  36.1 0.0 slice-start
  36.1 1.7 fusion
  37.8 33.3 %psum.7 = f32[512]{0:T(512)S(1)} all-reduce(f32[512]{0:T(512)S(1)} %fusion), channel_id=1, replica_groups=mesh['wa'=16,'ha'=8] {'wa'}, use_global_device_ids=true, to_apply=%region_1.0 | all-reduce | flops 512 | bytes 4096 | tf_op jit(solution)/shard_map/psum | solution.py:22
  71.1 0.0 copy-start
  71.1 0.0 slice-start.1
  71.1 0.0 copy-start.1
  71.1 6.7 %fusion.4 = f32[512,3328]{1,0:T(8,128)S(1)} fusion(bf16[1024,3328]{1,0:T(8,128)(2,1)} %param.8, bf16[512,1024]{1,0:T(8,128)(2,1)} %all-gather.3.cloned.1.call-done, f32[1024]{0:T(1024)} %param.6, f32[512]{0:T(512)S(1)} %add_rsqrt_fusion), kind=kOutput, calls=%fused_computation.8 | convolution fusion | flops 3491758080 | bytes 14686208 | tf_op jit(solution)/shard_map/dot_general | solution.py:26
  77.9 0.0 slice-done
  77.9 0.0 copy-done
  77.9 0.0 slice-done.1
  77.9 0.0 copy-done.1
  77.9 3.8 %fusion.6 = f32[512,3328]{1,0:T(8,128)S(1)} fusion(bf16[1024,3328]{1,0:T(8,128)(2,1)S(1)} %bitcast.5, bf16[512,1024]{1,0:T(8,128)(2,1)S(1)} %copy-done, f32[1024]{0:T(1024)S(1)} %copy-done.1, f32[512]{0:T(512)S(1)} %add_rsqrt_fusion), kind=kOutput, calls=%fused_computation.9 | convolution fusion | flops 3491758080 | bytes 14686208 | tf_op jit(solution)/shard_map/dot_general | solution.py:25
  81.7 5.4 %pad_maximum_fusion = f32[512,6656]{1,0:T(8,128)} fusion(f32[512,3328]{1,0:T(8,128)S(1)} %fusion.4, f32[512,3328]{1,0:T(8,128)S(1)} %fusion.6), kind=kLoop, calls=%fused_computation | loop fusion | flops 3407872 | bytes 27262976 | tf_op jit(solution)/shard_map/concatenate | solution.py:28
  87.2 0.0 reduce-scatter.3.cloned.1.call-update
  87.2 0.0 all-gather.5.cloned.1.call-start
  87.3 99.2 %reduce-scatter.3.cloned.1.call-done = f32[32,6656]{1,0:T(8,128)} async-done(((f32[512,6656]{1,0:T(8,128)}), f32[32,6656]{1,0:T(8,128)}) %reduce-scatter.3.cloned.1.call-update) | async-done | bytes 851984 | tf_op jit(solution)/shard_map/reduce_scatter | solution.py:27
  186.4 1.9 fusion.3
  188.4 0.0 all-gather.5.cloned.1.call-update
  188.4 0.0 reduce-scatter.5.cloned.1.call-start
  188.5 48.0 %all-gather.5.cloned.1.call-done = bf16[512,3328]{1,0:T(8,128)(2,1)} async-done(((bf16[32,3328]{1,0:T(8,128)(2,1)}), bf16[512,3328]{1,0:T(8,128)(2,1)}) %all-gather.5.cloned.1.call-update) | async-done | bytes 3407888 | tf_op jit(solution)/shard_map/all_gather | solution.py:32
  236.5 9.0 %fusion.8 = f32[512,1024]{1,0:T(8,128)} fusion(bf16[512,3328]{1,0:T(8,128)(2,1)} %all-gather.5.cloned.1.call-done, bf16[3328,1024]{1,0:T(8,128)(2,1)} %param.9), kind=kOutput, calls=%fused_computation.11 | convolution fusion | flops 3489660928 | bytes 12320768 | tf_op jit(solution)/shard_map/dot_general | solution.py:31
  245.5 0.0 reduce-scatter.5.cloned.1.call-update
  245.5 29.9 %reduce-scatter.5.cloned.1.call-done = f32[64,1024]{1,0:T(8,128)} async-done(((f32[512,1024]{1,0:T(8,128)}), f32[64,1024]{1,0:T(8,128)}) %reduce-scatter.5.cloned.1.call-update) | async-done | bytes 262160 | tf_op jit(solution)/shard_map/reduce_scatter | solution.py:36
  275.4 1.6 convert_element_type.15
  (2 shorter events, 0.0 us)
Async XLA Ops:
  6.5 29.6 %all-gather.3.cloned.1.call-start = ((), (), s32[]{:S(2)}) async-start(), calls=%async_computation.2 | async-start | bytes 1179648 | tf_op jit(solution)/shard_map/all_gather | solution.py:20
  7.3 179.2 %reduce-scatter.3.cloned.1.call-start = ((), (), s32[]{:S(2)}) async-start(), calls=%async_computation.3 | async-start | bytes 14483456 | tf_op jit(solution)/shard_map/reduce_scatter | solution.py:27
  36.1 41.8 %slice-start = ((s8[6815744]{0:T(1024)(128)(4,1)}), s8[2621440]{0:T(1024)(128)(4,1)S(1)}, s32[]{:S(2)}) async-start(s8[6815744]{0:T(1024)(128)(4,1)} %bitcast.4), calls=%async_computation.6 | async-start | bytes 5242880
  71.1 6.8 %copy-start = (bf16[512,1024]{1,0:T(8,128)(2,1)S(1)}, bf16[512,1024]{1,0:T(8,128)(2,1)}, u32[]{:S(2)}) copy-start(bf16[512,1024]{1,0:T(8,128)(2,1)} %all-gather.3.cloned.1.call-done) | copy-start | bytes 3145732
  71.1 6.8 %slice-start.1 = ((s8[6815744]{0:T(1024)(128)(4,1)}), s8[4194304]{0:T(1024)(128)(4,1)S(1)}, s32[]{:S(2)}) async-start(s8[6815744]{0:T(1024)(128)(4,1)} %bitcast.4), calls=%async_computation.7 | async-start | bytes 8388608
  71.1 6.8 %copy-start.1 = (f32[1024]{0:T(1024)S(1)}, f32[1024]{0:T(1024)}, u32[]{:S(2)}) copy-start(f32[1024]{0:T(1024)} %param.6) | copy-start | bytes 12292
  87.2 149.2 %all-gather.5.cloned.1.call-start = ((), (), s32[]{:S(2)}) async-start(), calls=%async_computation.4 | async-start | bytes 3620864 | tf_op jit(solution)/shard_map/all_gather | solution.py:32
  188.4 87.0 %reduce-scatter.5.cloned.1.call-start = ((), (), s32[]{:S(2)}) async-start(), calls=%async_computation.5 | async-start | bytes 2359296 | tf_op jit(solution)/shard_map/reduce_scatter | solution.py:36
Sparse Core Ops, SparseCore 0:
  9.1 26.9 all-gather.2
  87.3 99.0 reduce-scatter.2
  188.9 47.5 all-gather.4
  245.6 29.7 reduce-scatter.4
where the time goes:
time: 286 us; the launch traced here: 284 us
  waiting for transfers between devices  207 us (72%)
  blocking collectives  33.3 us (12%)
  matrix products  19.5 us (7%)
  between operations  13.2 us (5%)
  other arithmetic  10.7 us (4%)
    reduce_scatter x1, waiting for transfers between devices, body(): lax.psum_scatter(jnp.concatenate([gate_part, up_part], axis=1), 'wa', sca...  99.2 us
    all_gather x1, waiting for transfers between devices, body(): lax.all_gather(hidden, 'wa', axis=0, tiled=True)  48 us
    psum x1, blocking collectives, body(): squares = lax.psum(jnp.sum(own_values * own_values, axis=1), 'wa')  33.3 us
    reduce_scatter x1, waiting for transfers between devices, body(): lax.psum_scatter(partial_out, 'ha', scatter_dimension=0, tiled=True)  29.9 us
    all_gather x1, waiting for transfers between devices, body(): gathered = lax.all_gather(tokens, 'ha', axis=0, tiled=True)  28.8 us
    dot_general x1, matrix products, body(): jnp.dot(lax.all_gather(hidden, 'wa', axis=0, tiled=True), down_weight, pr...  9.01 us
    dot_general x1, matrix products, body(): up_part = jnp.dot(normed, up_weight, preferred_element_type=jnp.float32)  6.72 us
  transfers between devices with their start and end apart: 4, of which 4 were waited for; matrix products, arithmetic and copies ran while one was open for 0% of the time, Pallas kernels for 0%

commit v1 on v0

v1 whole, which is shorter than its diff:
```python
import jax
import jax.numpy as jnp
from jax import lax
from jax.sharding import PartitionSpec as P


def activate(summed, hidden_width, model_width):
    gate = summed[:, :hidden_width]
    up = summed[:, hidden_width:2 * hidden_width]
    squares = summed[:, 2 * hidden_width:2 * hidden_width + 1]
    scale = lax.rsqrt(squares / model_width + 1e-05)
    return (jax.nn.silu(gate * scale) * (up * scale)).astype(jnp.bfloat16)


def body(tokens, norm_gain, gate_weight, up_weight, down_weight):
    gathered = lax.all_gather(tokens, "ha", axis=0, tiled=True)
    own_values = gathered.astype(jnp.float32)
    model_width = own_values.shape[1] * lax.axis_size("wa")
    squares = jnp.sum(own_values * own_values, axis=1, keepdims=True)
    scaled = (own_values * norm_gain[None, :]).astype(jnp.bfloat16)
    hidden_width = gate_weight.shape[1]
    gate_part = jnp.dot(scaled, gate_weight, preferred_element_type=jnp.float32)
    up_part = jnp.dot(scaled, up_weight, preferred_element_type=jnp.float32)
    square_block = jnp.broadcast_to(squares, (squares.shape[0], 128))
    summed = lax.psum_scatter(
        jnp.concatenate([gate_part, up_part, square_block], axis=1), "wa", scatter_dimension=0, tiled=True
    )
    hidden = activate(summed, hidden_width, model_width)
    partial_out = jnp.dot(
        lax.all_gather(hidden, "wa", axis=0, tiled=True),
        down_weight,
        preferred_element_type=jnp.float32,
    )
    mixed_out = lax.psum_scatter(partial_out, "ha", scatter_dimension=0, tiled=True)
    return mixed_out.astype(jnp.bfloat16)


def solution(mesh):
    placed = (P("ha", "wa"), P("wa"), P("wa", "ha"), P("wa", "ha"), P("ha", "wa"))
    return jax.shard_map(body, mesh=mesh, in_specs=placed, out_specs=P("ha", "wa"), check_vma=False)
```

time: 286 us -> 252 us (0.88)
  blocking collectives: 33.3 us -> 0 us
    psum x1 -> x0, blocking collectives: 33.3 us -> none  [body(): squares = lax.psum(jnp.sum(own_values * own_values, axis=1), 'wa')]
where the time goes in v1:
time: 252 us; the launch traced here: 250 us
  waiting for transfers between devices  205 us (81%)
  matrix products  20 us (8%)
  between operations  13.2 us (5%)
  other arithmetic  11.4 us (5%)
    reduce_scatter x1, waiting for transfers between devices, body(): lax.psum_scatter(jnp.concatenate([gate_part, up_part, square_block], axis...  98 us
    all_gather x1, waiting for transfers between devices, body(): lax.all_gather(hidden, 'wa', axis=0, tiled=True)  47.6 us
    reduce_scatter x1, waiting for transfers between devices, body(): lax.psum_scatter(partial_out, 'ha', scatter_dimension=0, tiled=True)  29.9 us
    all_gather x1, waiting for transfers between devices, body(): gathered = lax.all_gather(tokens, 'ha', axis=0, tiled=True)  28.8 us
    dot_general x1, matrix products, body(): jnp.dot(lax.all_gather(hidden, 'wa', axis=0, tiled=True), down_weight, pr...  9.01 us
    dot_general x1, matrix products, body(): up_part = jnp.dot(scaled, up_weight, preferred_element_type=jnp.float32)  7.28 us
    concatenate x1, other arithmetic, body(): jnp.concatenate([gate_part, up_part, square_block], axis=1)  5.25 us
  transfers between devices with their start and end apart: 4, of which 4 were waited for; matrix products, arithmetic and copies ran while one was open for 0% of the time, Pallas kernels for 0%

profile of v1, /device:TPU:1, one launch (start us, length us, event | category | flops | bytes accessed | tf_op | source)
XLA Modules:
  0.0 249.9 jit_solution(16157814636659487597)
XLA Ops:
  6.5 0.0 all-gather.3.cloned.1.call-start
  6.5 0.7 all-gather.3.cloned.1.call-update
  7.3 0.0 reduce-scatter.3.cloned.1.call-start
  7.3 28.8 %all-gather.3.cloned.1.call-done = bf16[512,1024]{1,0:T(8,128)(2,1)} async-done(((bf16[64,1024]{1,0:T(8,128)(2,1)}), bf16[512,1024]{1,0:T(8,128)(2,1)}) %all-gather.3.cloned.1.call-update) | async-done | bytes 1048592 | tf_op jit(solution)/shard_map/all_gather | solution.py:16
  36.1 0.0 slice-start
  36.1 1.7 fusion.1
  37.8 0.0 copy-start
  37.8 0.0 slice-start.1
  37.8 0.0 copy-start.1
  37.8 7.3 %fusion.2 = f32[512,3328]{1,0:T(8,128)S(1)} fusion(bf16[1024,3328]{1,0:T(8,128)(2,1)} %param.8, bf16[512,1024]{1,0:T(8,128)(2,1)} %all-gather.3.cloned.1.call-done, f32[1024]{0:T(1024)} %param.6), kind=kOutput, calls=%fused_computation.5 | convolution fusion | flops 3491233792 | bytes 14684160 | tf_op jit(solution)/shard_map/dot_general | solution.py:23
  45.1 0.0 slice-done
  45.1 0.0 copy-done
  45.1 0.0 slice-done.1
  45.1 0.0 copy-done.1
  45.1 3.7 %fusion.4 = f32[512,3328]{1,0:T(8,128)S(1)} fusion(bf16[1024,3328]{1,0:T(8,128)(2,1)S(1)} %bitcast.5, bf16[512,1024]{1,0:T(8,128)(2,1)S(1)} %copy-done, f32[1024]{0:T(1024)S(1)} %copy-done.1), kind=kOutput, calls=%fused_computation.6 | convolution fusion | flops 3491233792 | bytes 14684160 | tf_op jit(solution)/shard_map/dot_general | solution.py:22
  48.9 0.1 broadcast_in_dim.2
  49.0 5.3 %pad_maximum_fusion = f32[512,6784]{1,0:T(8,128)} fusion(f32[512,128]{1,0:T(8,128)S(1)} %broadcast_in_dim.2, f32[512,3328]{1,0:T(8,128)S(1)} %fusion.2, f32[512,3328]{1,0:T(8,128)S(1)} %fusion.4), kind=kLoop, calls=%fused_computation | loop fusion | flops 6946816 | bytes 27787264 | tf_op jit(solution)/shard_map/concatenate | solution.py:26
  54.2 0.0 reduce-scatter.3.cloned.1.call-update
  54.3 0.0 all-gather.5.cloned.1.call-start
  54.3 98.0 %reduce-scatter.3.cloned.1.call-done = f32[32,6784]{1,0:T(8,128)} async-done(((f32[512,6784]{1,0:T(8,128)}), f32[32,6784]{1,0:T(8,128)}) %reduce-scatter.3.cloned.1.call-update) | async-done | bytes 868368 | tf_op jit(solution)/shard_map/reduce_scatter | solution.py:25
  152.3 0.8 fusion.10
  153.1 2.0 fusion.7
  155.1 0.0 all-gather.5.cloned.1.call-update
  155.2 0.0 reduce-scatter.5.cloned.1.call-start
  155.2 47.6 %all-gather.5.cloned.1.call-done = bf16[512,3328]{1,0:T(8,128)(2,1)} async-done(((bf16[32,3328]{1,0:T(8,128)(2,1)}), bf16[512,3328]{1,0:T(8,128)(2,1)}) %all-gather.5.cloned.1.call-update) | async-done | bytes 3407888 | tf_op jit(solution)/shard_map/all_gather | solution.py:30
  202.8 9.0 %fusion.11 = f32[512,1024]{1,0:T(8,128)} fusion(bf16[512,3328]{1,0:T(8,128)(2,1)} %all-gather.5.cloned.1.call-done, bf16[3328,1024]{1,0:T(8,128)(2,1)} %param.9), kind=kOutput, calls=%fused_computation.15 | convolution fusion | flops 3489660928 | bytes 12320768 | tf_op jit(solution)/shard_map/dot_general | solution.py:29
  211.8 0.0 reduce-scatter.5.cloned.1.call-update
  211.9 29.9 %reduce-scatter.5.cloned.1.call-done = f32[64,1024]{1,0:T(8,128)} async-done(((f32[512,1024]{1,0:T(8,128)}), f32[64,1024]{1,0:T(8,128)}) %reduce-scatter.5.cloned.1.call-update) | async-done | bytes 262160 | tf_op jit(solution)/shard_map/reduce_scatter | solution.py:34
  241.8 1.6 convert_element_type.15
  (1 shorter events, 0.0 us)
Async XLA Ops:
  6.5 29.6 %all-gather.3.cloned.1.call-start = ((), (), s32[]{:S(2)}) async-start(), calls=%async_computation.2 | async-start | bytes 1179648 | tf_op jit(solution)/shard_map/all_gather | solution.py:16
  7.3 145.0 %reduce-scatter.3.cloned.1.call-start = ((), (), s32[]{:S(2)}) async-start(), calls=%async_computation.3 | async-start | bytes 14761984 | tf_op jit(solution)/shard_map/reduce_scatter | solution.py:25
  36.1 9.0 %slice-start = ((s8[6815744]{0:T(1024)(128)(4,1)}), s8[4194304]{0:T(1024)(128)(4,1)S(1)}, s32[]{:S(2)}) async-start(s8[6815744]{0:T(1024)(128)(4,1)} %bitcast.4), calls=%async_computation.6 | async-start | bytes 8388608
  37.8 7.3 %copy-start = (bf16[512,1024]{1,0:T(8,128)(2,1)S(1)}, bf16[512,1024]{1,0:T(8,128)(2,1)}, u32[]{:S(2)}) copy-start(bf16[512,1024]{1,0:T(8,128)(2,1)} %all-gather.3.cloned.1.call-done) | copy-start | bytes 3145732
  37.8 7.3 %slice-start.1 = ((s8[6815744]{0:T(1024)(128)(4,1)}), s8[2621440]{0:T(1024)(128)(4,1)S(1)}, s32[]{:S(2)}) async-start(s8[6815744]{0:T(1024)(128)(4,1)} %bitcast.4), calls=%async_computation.7 | async-start | bytes 5242880
  37.8 7.3 %copy-start.1 = (f32[1024]{0:T(1024)S(1)}, f32[1024]{0:T(1024)}, u32[]{:S(2)}) copy-start(f32[1024]{0:T(1024)} %param.6) | copy-start | bytes 12292
  54.3 148.6 %all-gather.5.cloned.1.call-start = ((), (), s32[]{:S(2)}) async-start(), calls=%async_computation.4 | async-start | bytes 3620864 | tf_op jit(solution)/shard_map/all_gather | solution.py:30
  155.2 86.6 %reduce-scatter.5.cloned.1.call-start = ((), (), s32[]{:S(2)}) async-start(), calls=%async_computation.5 | async-start | bytes 2359296 | tf_op jit(solution)/shard_map/reduce_scatter | solution.py:34
Sparse Core Ops, SparseCore 0:
  9.1 26.9 all-gather.2
  54.4 97.8 reduce-scatter.2
  155.3 47.4 all-gather.4
  212.0 29.7 reduce-scatter.4

commit v2 on v1

v2 whole, which is shorter than its diff:
```python
import functools

import jax
import jax.numpy as jnp
from jax import lax
from jax.experimental import pallas as pl
from jax.experimental.pallas import tpu as pltpu
from jax.sharding import PartitionSpec as P

MESH = pl.DeviceIdType.MESH


def _greet(axis, n, me):
    barrier = pltpu.get_barrier_semaphore()
    for k in range(1, n):
        pl.semaphore_signal(barrier, inc=1, device_id={axis: lax.rem(me + k, n)}, device_id_type=MESH)
    pl.semaphore_wait(barrier, n - 1)


def _exchange_kernel(mode, axis, n, rows, x_ref, out_ref, slots, send_sem, recv_sem):
    me = lax.axis_index(axis)
    _greet(axis, n, me)
    copies = []
    for k in range(1, n):
        peer = lax.rem(me + k, n)
        if mode == "gather":
            source = x_ref
        elif mode == "scatter":
            source = x_ref.at[pl.ds(pl.multiple_of(peer * rows, rows), rows)]
        else:
            source = x_ref
        copy = pltpu.make_async_remote_copy(
            src_ref=source,
            dst_ref=slots.at[k],
            send_sem=send_sem.at[k],
            recv_sem=recv_sem.at[k],
            device_id={axis: peer},
            device_id_type=MESH,
        )
        copy.start()
        copies.append(copy)
    if mode == "gather":
        out_ref[pl.ds(pl.multiple_of(me * rows, rows), rows), :] = x_ref[...]
        for k, copy in enumerate(copies, 1):
            copy.wait()
            sender = lax.rem(me + n - k, n)
            out_ref[pl.ds(pl.multiple_of(sender * rows, rows), rows), :] = slots[k]
    elif mode == "scatter":
        total = x_ref[pl.ds(pl.multiple_of(me * rows, rows), rows), :].astype(jnp.float32)
        for k, copy in enumerate(copies, 1):
            copy.wait()
            total = total + slots[k].astype(jnp.float32)
        out_ref[...] = total
    else:
        for copy in copies:
            copy.wait()
        slots[0] = x_ref[...]
        total = jnp.zeros(out_ref.shape, jnp.float32)
        for sender in range(n):
            total = total + slots[lax.rem(me + n - sender, n)].astype(jnp.float32)
        out_ref[...] = total


def exchange(x, mode, axis, n, collective_id):
    if mode == "gather":
        rows = x.shape[0]
        out_shape = jax.ShapeDtypeStruct((n * rows, x.shape[1]), x.dtype)
    elif mode == "scatter":
        rows = x.shape[0] // n
        out_shape = jax.ShapeDtypeStruct((rows, x.shape[1]), jnp.float32)
    else:
        rows = x.shape[0]
        out_shape = jax.ShapeDtypeStruct(x.shape, jnp.float32)
    return pl.pallas_call(
        functools.partial(_exchange_kernel, mode, axis, n, rows),
        out_shape=out_shape,
        in_specs=[pl.BlockSpec(memory_space=pltpu.VMEM)],
        out_specs=pl.BlockSpec(memory_space=pltpu.VMEM),
        scratch_shapes=[
            pltpu.VMEM((n, rows, x.shape[1]), x.dtype),
            pltpu.SemaphoreType.DMA((n,)),
            pltpu.SemaphoreType.DMA((n,)),
        ],
        compiler_params=pltpu.CompilerParams(collective_id=collective_id, has_side_effects=True),
    )(x)


def body(tokens, norm_gain, gate_weight, up_weight, down_weight):
    n_wa = lax.axis_size("wa")
    n_ha = lax.axis_size("ha")
    own_values = tokens.astype(jnp.float32)
    model_width = own_values.shape[1] * n_wa
    own_rows = own_values.shape[0]
    partial_squares = jnp.sum(own_values * own_values, axis=1)
    packed = jnp.pad(partial_squares.reshape(8, own_rows // 8), ((0, 0), (0, 128 - own_rows // 8)))
    squares = exchange(packed, "sum", "wa", n_wa, 0)[:, : own_rows // 8].reshape(own_rows, 1)
    mean_square = squares / model_width
    normed = (own_values * lax.rsqrt(mean_square + 1e-05) * norm_gain[None, :]).astype(jnp.bfloat16)
    gathered = exchange(normed, "gather", "ha", n_ha, 1)
    hidden_width = gate_weight.shape[1]
    gate_part = jnp.dot(gathered, gate_weight, preferred_element_type=jnp.float32)
    up_part = jnp.dot(gathered, up_weight, preferred_element_type=jnp.float32)
    both = jnp.concatenate([gate_part, up_part], axis=1).astype(jnp.bfloat16)
    summed = exchange(both, "scatter", "wa", n_wa, 2)
    gate = summed[:, :hidden_width]
    up = summed[:, hidden_width:]
    hidden = (jax.nn.silu(gate) * up).astype(jnp.bfloat16)
    all_hidden = exchange(hidden, "gather", "wa", n_wa, 3)
    partial_out = jnp.dot(all_hidden, down_weight, preferred_element_type=jnp.float32)
    mixed_out = exchange(partial_out, "scatter", "ha", n_ha, 4)
    return mixed_out.astype(jnp.bfloat16)


def solution(mesh):
    placed = (P("ha", "wa"), P("wa"), P("wa", "ha"), P("wa", "ha"), P("ha", "wa"))
    return jax.shard_map(body, mesh=mesh, in_specs=placed, out_specs=P("ha", "wa"), check_vma=False)
```

time: 252 us -> 328 us (1.30); the launches traced: 250 us -> 322 us
  Pallas kernels: 0 us -> 288 us
  waiting for transfers between devices: 205 us -> 0 us
  between operations: 13.2 us -> 0.08 us
    pallas_call x0 -> x5, Pallas kernels: none -> 288 us  [exchange(): pl.pallas_call(functools.partial(_exchange_kernel, mode, axis, n, rows),...]
    reduce_scatter x2 -> x0, waiting for transfers between devices: 128 us -> none  [the longest x1 98 us: body(): lax.psum_scatter(jnp.concatenate([gate_part, up_part, square_block], axis...]
    all_gather x2 -> x0, waiting for transfers between devices: 76.4 us -> none  [the longest x1 47.6 us: body(): lax.all_gather(hidden, 'wa', axis=0, tiled=True)]
  transfers between devices with their start and end apart: 4 -> 0, of which waited for: 4 -> 0; matrix products, arithmetic and copies ran while one was open for 0% -> 0% of each run, Pallas kernels for 0% -> 0%
where the time goes in v2:
time: 328 us; the launch traced here: 322 us
  Pallas kernels  288 us (88%)
  matrix products  22.9 us (7%)
  other arithmetic  10.2 us (3%)
    pallas_call x5, Pallas kernels, exchange(): pl.pallas_call(functools.partial(_exchange_kernel, mode, axis, n, rows),...  288 us
    dot_general x1, matrix products, body(): jnp.dot(all_hidden, down_weight, preferred_element_type=jnp.float32)  9.02 us
    dot_general x1, matrix products, body(): up_part = jnp.dot(gathered, up_weight, preferred_element_type=jnp.float32)  7.02 us
    dot_general x1, matrix products, body(): jnp.dot(gathered, gate_weight, preferred_element_type=jnp.float32)  6.88 us

profile of v2, /device:TPU:1, one launch (start us, length us, event | category | flops | bytes accessed | tf_op | source)
XLA Modules:
  0.0 321.9 jit_solution(520889617768845391)
XLA Ops:
  0.0 1.0 fusion
  1.0 0.1 reshape.21
  1.1 0.6 pad.4.x_ref
  1.7 11.7 %shard_map.55 = f32[8,128]{1,0:T(8,128)} custom-call(f32[8,128]{1,0:T(8,128)} %pad.4.x_ref), custom_call_target="tpu_custom_call" | custom-call | tf_op jit(solution)/shard_map/pallas_call | solution.py:74
  13.4 0.7 add_rsqrt_fusion
  14.1 0.1 rsqrt.12
  14.2 1.7 fusion.2.x_ref
  15.9 19.9 %shard_map.56 = bf16[512,1024]{1,0:T(8,128)(2,1)} custom-call(bf16[64,1024]{1,0:T(8,128)(2,1)} %fusion.2.x_ref), custom_call_target="tpu_custom_call" | custom-call | tf_op jit(solution)/shard_map/pallas_call | solution.py:74
  35.8 0.0 copy-start
  35.8 7.0 %convolution_convert_fusion = bf16[512,3328]{1,0:T(8,128)(2,1)S(1)} fusion(bf16[512,1024]{1,0:T(8,128)(2,1)} %shard_map.56, bf16[1024,3328]{1,0:T(8,128)(2,1)} %param.8), kind=kOutput, calls=%fused_computation.1 | convolution fusion | flops 3491364864 | bytes 11272192 | tf_op jit(solution)/shard_map/dot_general | solution.py:102
  42.8 0.0 copy-done
  42.8 6.9 %convolution_convert_fusion.1 = bf16[512,3328]{1,0:T(8,128)(2,1)S(1)} fusion(bf16[512,1024]{1,0:T(8,128)(2,1)S(1)} %copy-done, bf16[1024,3328]{1,0:T(8,128)(2,1)} %param.7), kind=kOutput, calls=%fused_computation.2 | convolution fusion | flops 3491364864 | bytes 11272192 | tf_op jit(solution)/shard_map/dot_general | solution.py:101
  49.7 3.3 %pad_maximum_fusion.x_ref = bf16[512,6656]{1,0:T(8,128)(2,1)} fusion(bf16[512,3328]{1,0:T(8,128)(2,1)S(1)} %convolution_convert_fusion, bf16[512,3328]{1,0:T(8,128)(2,1)S(1)} %convolution_convert_fusion.1), kind=kLoop, calls=%fused_computation | loop fusion | flops 13631488 | bytes 13631488 | tf_op jit(solution)/shard_map/concatenate | solution.py:103
  53.0 135.9 %shard_map.57 = f32[32,6656]{1,0:T(8,128)} custom-call(bf16[512,6656]{1,0:T(8,128)(2,1)} %pad_maximum_fusion.x_ref), custom_call_target="tpu_custom_call" | custom-call | tf_op jit(solution)/shard_map/pallas_call | solution.py:74
  188.9 1.9 multiply_convert_fusion.x_ref
  190.8 89.9 %shard_map.58 = bf16[512,3328]{1,0:T(8,128)(2,1)} custom-call(bf16[32,3328]{1,0:T(8,128)(2,1)} %multiply_convert_fusion.x_ref), custom_call_target="tpu_custom_call" | custom-call | tf_op jit(solution)/shard_map/pallas_call | solution.py:74
  280.8 9.0 %fusion.3.x_ref = f32[512,1024]{1,0:T(8,128)} fusion(bf16[512,3328]{1,0:T(8,128)(2,1)} %shard_map.58, bf16[3328,1024]{1,0:T(8,128)(2,1)} %param.9), kind=kOutput, calls=%fused_computation.10 | convolution fusion | flops 3489660928 | bytes 12320768 | tf_op jit(solution)/shard_map/dot_general | solution.py:109
  289.8 30.4 %shard_map.59 = f32[64,1024]{1,0:T(8,128)} custom-call(f32[512,1024]{1,0:T(8,128)} %fusion.3.x_ref), custom_call_target="tpu_custom_call" | custom-call | tf_op jit(solution)/shard_map/pallas_call | solution.py:74
  320.2 1.6 convert_element_type.18
Async XLA Ops:
  35.8 7.0 %copy-start = (bf16[512,1024]{1,0:T(8,128)(2,1)S(1)}, bf16[512,1024]{1,0:T(8,128)(2,1)}, u32[]{:S(2)}) copy-start(bf16[512,1024]{1,0:T(8,128)(2,1)} %shard_map.56) | copy-start | bytes 3145732

commit v3 on v2

--- a/solution.py
+++ b/solution.py
@@ -100,14 +100,15 @@
     hidden_width = gate_weight.shape[1]
     gate_part = jnp.dot(gathered, gate_weight, preferred_element_type=jnp.float32)
     up_part = jnp.dot(gathered, up_weight, preferred_element_type=jnp.float32)
-    both = jnp.concatenate([gate_part, up_part], axis=1).astype(jnp.bfloat16)
-    summed = exchange(both, "scatter", "wa", n_wa, 2)
+    summed = lax.psum_scatter(
+        jnp.concatenate([gate_part, up_part], axis=1), "wa", scatter_dimension=0, tiled=True
+    )
     gate = summed[:, :hidden_width]
     up = summed[:, hidden_width:]
     hidden = (jax.nn.silu(gate) * up).astype(jnp.bfloat16)
-    all_hidden = exchange(hidden, "gather", "wa", n_wa, 3)
+    all_hidden = lax.all_gather(hidden, "wa", axis=0, tiled=True)
     partial_out = jnp.dot(all_hidden, down_weight, preferred_element_type=jnp.float32)
-    mixed_out = exchange(partial_out, "scatter", "ha", n_ha, 4)
+    mixed_out = exchange(partial_out.astype(jnp.bfloat16), "scatter", "ha", n_ha, 4)
     return mixed_out.astype(jnp.bfloat16)
 
 

time: 328 us -> 241 us (0.73); the launches traced: 322 us -> 241 us
  Pallas kernels: 288 us -> 50.6 us
  waiting for transfers between devices: 0 us -> 144 us
  between operations: 0.08 us -> 13.5 us
  matrix products: 22.9 us -> 19.6 us
    pallas_call x5 -> x3, Pallas kernels: 288 us -> 50.6 us  [exchange(): pl.pallas_call(functools.partial(_exchange_kernel, mode, axis, n, rows),...]
    reduce_scatter x0 -> x1, waiting for transfers between devices: none -> 96.1 us  [body(): lax.psum_scatter(jnp.concatenate([gate_part, up_part], axis=1), 'wa', sca...]
    all_gather x0 -> x1, waiting for transfers between devices: none -> 48 us  [body(): all_hidden = lax.all_gather(hidden, 'wa', axis=0, tiled=True)]
  transfers between devices with their start and end apart: 0 -> 2, of which waited for: 0 -> 2; matrix products, arithmetic and copies ran while one was open for 0% -> 0% of each run, Pallas kernels for 0% -> 0%
where the time goes in v3:
time: 241 us
  waiting for transfers between devices  144 us (60%)
  Pallas kernels  50.6 us (21%)
  matrix products  19.6 us (8%)
  between operations  13.5 us (6%)
  other arithmetic  12.4 us (5%)
    reduce_scatter x1, waiting for transfers between devices, body(): lax.psum_scatter(jnp.concatenate([gate_part, up_part], axis=1), 'wa', sca...  96.1 us
    pallas_call x3, Pallas kernels, exchange(): pl.pallas_call(functools.partial(_exchange_kernel, mode, axis, n, rows),...  50.6 us
    all_gather x1, waiting for transfers between devices, body(): all_hidden = lax.all_gather(hidden, 'wa', axis=0, tiled=True)  48 us
    dot_general x1, matrix products, body(): jnp.dot(all_hidden, down_weight, preferred_element_type=jnp.float32)  8.63 us
    dot_general x1, matrix products, body(): up_part = jnp.dot(gathered, up_weight, preferred_element_type=jnp.float32)  7.26 us
    concatenate x1, other arithmetic, body(): jnp.concatenate([gate_part, up_part], axis=1)  5.46 us
  transfers between devices with their start and end apart: 2, of which 2 were waited for; matrix products, arithmetic and copies ran while one was open for 0% of the time, Pallas kernels for 0%

profile of v3, /device:TPU:1, one launch (start us, length us, event | category | flops | bytes accessed | tf_op | source)
XLA Modules:
  0.0 241.0 jit_solution(7832403702237794605)
XLA Ops:
  6.5 0.0 reduce-scatter.2.cloned.1.call-start
  6.5 1.0 fusion.1
  7.6 0.1 reshape.21
  7.6 0.6 pad.4.x_ref
  8.3 11.7 %shard_map.55 = f32[8,128]{1,0:T(8,128)} custom-call(f32[8,128]{1,0:T(8,128)} %pad.4.x_ref), custom_call_target="tpu_custom_call" | custom-call | tf_op jit(solution)/shard_map/pallas_call | solution.py:74
  20.0 0.7 add_rsqrt_fusion
  20.7 0.1 rsqrt.12
  20.7 1.7 fusion.3.x_ref
  22.4 0.0 slice-start
  22.4 20.0 %shard_map.56 = bf16[512,1024]{1,0:T(8,128)(2,1)} custom-call(bf16[64,1024]{1,0:T(8,128)(2,1)} %fusion.3.x_ref), custom_call_target="tpu_custom_call" | custom-call | tf_op jit(solution)/shard_map/pallas_call | solution.py:74
  42.4 0.0 copy-start
  42.4 0.0 slice-start.1
  42.5 7.3 %fusion.5 = f32[512,3328]{1,0:T(8,128)S(1)} fusion(bf16[512,1024]{1,0:T(8,128)(2,1)} %shard_map.56, bf16[1024,3328]{1,0:T(8,128)(2,1)} %param.8), kind=kOutput, calls=%fused_computation.11 | convolution fusion | flops 3489660928 | bytes 14680064 | tf_op jit(solution)/shard_map/dot_general | solution.py:102
  49.7 0.0 slice-done
  49.7 0.0 copy-done
  49.7 0.0 slice-done.1
  49.8 3.7 %fusion.4 = f32[512,3328]{1,0:T(8,128)S(1)} fusion(bf16[512,1024]{1,0:T(8,128)(2,1)S(1)} %copy-done, bf16[1024,3328]{1,0:T(8,128)(2,1)S(1)} %bitcast.7), kind=kOutput, calls=%fused_computation.10 | convolution fusion | flops 3489660928 | bytes 14680064 | tf_op jit(solution)/shard_map/dot_general | solution.py:101
  53.5 5.5 %pad_maximum_fusion = f32[512,6656]{1,0:T(8,128)} fusion(f32[512,3328]{1,0:T(8,128)S(1)} %fusion.5, f32[512,3328]{1,0:T(8,128)S(1)} %fusion.4), kind=kLoop, calls=%fused_computation | loop fusion | flops 3407872 | bytes 27262976 | tf_op jit(solution)/shard_map/concatenate | solution.py:104
  58.9 0.0 reduce-scatter.2.cloned.1.call-update
  58.9 0.0 all-gather.2.cloned.1.call-start
  59.0 96.1 %reduce-scatter.2.cloned.1.call-done = f32[32,6656]{1,0:T(8,128)} async-done(((f32[512,6656]{1,0:T(8,128)}), f32[32,6656]{1,0:T(8,128)}) %reduce-scatter.2.cloned.1.call-update) | async-done | bytes 851984 | tf_op jit(solution)/shard_map/reduce_scatter | solution.py:103
  155.0 1.9 fusion
  157.0 0.0 all-gather.2.cloned.1.call-update
  157.0 48.0 %all-gather.2.cloned.1.call-done = bf16[512,3328]{1,0:T(8,128)(2,1)} async-done(((bf16[32,3328]{1,0:T(8,128)(2,1)}), bf16[512,3328]{1,0:T(8,128)(2,1)}) %all-gather.2.cloned.1.call-update) | async-done | bytes 3407888 | tf_op jit(solution)/shard_map/all_gather | solution.py:109
  205.0 8.6 %convolution_convert_fusion.x_ref = bf16[512,1024]{1,0:T(8,128)(2,1)} fusion(bf16[512,3328]{1,0:T(8,128)(2,1)} %all-gather.2.cloned.1.call-done, bf16[3328,1024]{1,0:T(8,128)(2,1)} %param.9), kind=kOutput, calls=%fused_computation.1 | convolution fusion | flops 3490185216 | bytes 11272192 | tf_op jit(solution)/shard_map/dot_general | solution.py:110
  213.7 18.9 %shard_map.57 = f32[64,1024]{1,0:T(8,128)} custom-call(bf16[512,1024]{1,0:T(8,128)(2,1)} %convolution_convert_fusion.x_ref), custom_call_target="tpu_custom_call" | custom-call | tf_op jit(solution)/shard_map/pallas_call | solution.py:74
  232.6 1.6 convert_element_type.21
  (1 shorter events, 0.0 us)
Async XLA Ops:
  6.5 148.5 %reduce-scatter.2.cloned.1.call-start = ((), (), s32[]{:S(2)}) async-start(), calls=%async_computation.1 | async-start | bytes 14483456 | tf_op jit(solution)/shard_map/reduce_scatter | solution.py:103
  22.4 27.3 %slice-start = ((s8[6815744]{0:T(1024)(128)(4,1)}), s8[2621440]{0:T(1024)(128)(4,1)S(1)}, s32[]{:S(2)}) async-start(s8[6815744]{0:T(1024)(128)(4,1)} %bitcast.6), calls=%async_computation.3 | async-start | bytes 5242880
  42.4 7.3 %copy-start = (bf16[512,1024]{1,0:T(8,128)(2,1)S(1)}, bf16[512,1024]{1,0:T(8,128)(2,1)}, u32[]{:S(2)}) copy-start(bf16[512,1024]{1,0:T(8,128)(2,1)} %shard_map.56) | copy-start | bytes 3145732
  42.4 7.3 %slice-start.1 = ((s8[6815744]{0:T(1024)(128)(4,1)}), s8[4194304]{0:T(1024)(128)(4,1)S(1)}, s32[]{:S(2)}) async-start(s8[6815744]{0:T(1024)(128)(4,1)} %bitcast.6), calls=%async_computation.4 | async-start | bytes 8388608
  58.9 146.1 %all-gather.2.cloned.1.call-start = ((), (), s32[]{:S(2)}) async-start(), calls=%async_computation.2 | async-start | bytes 3620864 | tf_op jit(solution)/shard_map/all_gather | solution.py:109
Sparse Core Ops, SparseCore 0:
  59.1 95.9 reduce-scatter.1
  157.5 47.5 all-gather.1

commit v4 on v3

--- a/solution.py
+++ b/solution.py
@@ -62,6 +62,8 @@
 
 
 def exchange(x, mode, axis, n, collective_id):
+    if n == 1:
+        return x.astype(jnp.float32) if mode != "gather" else x
     if mode == "gather":
         rows = x.shape[0]
         out_shape = jax.ShapeDtypeStruct((n * rows, x.shape[1]), x.dtype)
@@ -85,6 +87,110 @@
     )(x)
 
 
+def _ring_rs_kernel(side, cols, p_ref, out_ref, recv1, acc1, s1, recv2, acc2, send_sem, recv_sem):
+    w = lax.axis_index("wa")
+    x, z = w // side, lax.rem(w, side)
+
+    def peer(axis, delta):
+        if axis == 0:
+            return lax.rem(x + delta + side, side) * side + z
+        return x * side + lax.rem(z + delta + side, side)
+
+    barrier = pltpu.get_barrier_semaphore()
+    for axis in (0, 1):
+        for delta in (1, -1):
+            pl.semaphore_signal(barrier, inc=1, device_id={"wa": peer(axis, delta)}, device_id_type=MESH)
+    pl.semaphore_wait(barrier, 4)
+
+    flows = []
+    for f in range(4):
+        first = 0 if f < 2 else 1
+        delta = 1 if f % 2 == 0 else -1
+        flows.append((first, delta, pl.ds(f * cols, cols)))
+
+    def own1(f, chunk):
+        first, _, c = flows[f]
+        if first == 0:
+            return p_ref.at[chunk, :, :, c]
+        return p_ref.at[:, chunk, :, c]
+
+    def sem(stage, step, f):
+        return (stage * 3 + step) * 4 + f
+
+    sends = []
+    pos1 = [x if flows[f][0] == 0 else z for f in range(4)]
+    pos2 = [z if flows[f][0] == 0 else x for f in range(4)]
+    last = [None] * 4
+    for step in range(side - 1):
+        for f in range(4):
+            first, delta, _ = flows[f]
+            chunk = lax.rem(pos1[f] - delta * (step + 1) + 2 * side, side)
+            if step == 0:
+                source = own1(f, chunk)
+            else:
+                last[f].wait_recv()
+                acc1[f, step - 1] = recv1[f, step - 1] + own1(f, chunk)[...]
+                source = acc1.at[f, step - 1]
+            copy = pltpu.make_async_remote_copy(
+                src_ref=source, dst_ref=recv1.at[f, step],
+                send_sem=send_sem.at[sem(0, step, f)], recv_sem=recv_sem.at[sem(0, step, f)],
+                device_id={"wa": peer(first, delta)}, device_id_type=MESH)
+            copy.start()
+            sends.append(copy)
+            last[f] = copy
+    for f in range(4):
+        last[f].wait_recv()
+        s1[f] = recv1[f, side - 2] + own1(f, pos1[f])[...]
+    for step in range(side - 1):
+        for f in range(4):
+            first, delta, _ = flows[f]
+            chunk = lax.rem(pos2[f] - delta * (step + 1) + 2 * side, side)
+            if step == 0:
+                source = s1.at[f, chunk]
+            else:
+                last[f].wait_recv()
+                acc2[f, step - 1] = recv2[f, step - 1] + s1[f, chunk]
+                source = acc2.at[f, step - 1]
+            copy = pltpu.make_async_remote_copy(
+                src_ref=source, dst_ref=recv2.at[f, step],
+                send_sem=send_sem.at[sem(1, step, f)], recv_sem=recv_sem.at[sem(1, step, f)],
+                device_id={"wa": peer(1 - first, delta)}, device_id_type=MESH)
+            copy.start()
+            sends.append(copy)
+            last[f] = copy
+    for f in range(4):
+        last[f].wait_recv()
+        out_ref[:, flows[f][2]] = recv2[f, side - 2] + s1[f, pos2[f]]
+    for copy in sends:
+        copy.wait_send()
+
+
+def ring_reduce_scatter(partial, n, collective_id):
+    side = 4
+    rows = partial.shape[0] // n
+    width = partial.shape[1]
+    cols = width // 4
+    p4 = partial.reshape(side, side, rows, width)
+    f32 = jnp.float32
+    return pl.pallas_call(
+        functools.partial(_ring_rs_kernel, side, cols),
+        out_shape=jax.ShapeDtypeStruct((rows, width), f32),
+        in_specs=[pl.BlockSpec(memory_space=pltpu.VMEM)],
+        out_specs=pl.BlockSpec(memory_space=pltpu.VMEM),
+        scratch_shapes=[
+            pltpu.VMEM((4, side - 1, side, rows, cols), f32),
+            pltpu.VMEM((4, side - 2, side, rows, cols), f32),
+            pltpu.VMEM((4, side, rows, cols), f32),
+            pltpu.VMEM((4, side - 1, rows, cols), f32),
+            pltpu.VMEM((4, side - 2, rows, cols), f32),
+            pltpu.SemaphoreType.DMA((24,)),
+            pltpu.SemaphoreType.DMA((24,)),
+        ],
+        compiler_params=pltpu.CompilerParams(
+            collective_id=collective_id, has_side_effects=True, vmem_limit_bytes=60 * 1024 * 1024),
+    )(p4)
+
+
 def body(tokens, norm_gain, gate_weight, up_weight, down_weight):
     n_wa = lax.axis_size("wa")
     n_ha = lax.axis_size("ha")
@@ -100,9 +206,7 @@
     hidden_width = gate_weight.shape[1]
     gate_part = jnp.dot(gathered, gate_weight, preferred_element_type=jnp.float32)
     up_part = jnp.dot(gathered, up_weight, preferred_element_type=jnp.float32)
-    summed = lax.psum_scatter(
-        jnp.concatenate([gate_part, up_part], axis=1), "wa", scatter_dimension=0, tiled=True
-    )
+    summed = ring_reduce_scatter(jnp.concatenate([gate_part, up_part], axis=1), n_wa, 2)
     gate = summed[:, :hidden_width]
     up = summed[:, hidden_width:]
     hidden = (jax.nn.silu(gate) * up).astype(jnp.bfloat16)

time: 241 us -> 231 us (0.959)
  waiting for transfers between devices: 144 us -> 49.1 us
  Pallas kernels: 50.6 us -> 136 us
    reduce_scatter x1 -> x0, waiting for transfers between devices: 96.1 us -> none  [body(): lax.psum_scatter(jnp.concatenate([gate_part, up_part], axis=1), 'wa', sca...]
    pallas_call x0 -> x1, Pallas kernels: none -> 84.9 us  [ring_reduce_scatter(): pl.pallas_call(functools.partial(_ring_rs_kernel, side, cols), out_shape=...]
  transfers between devices with their start and end apart: 2 -> 1, of which waited for: 2 -> 1; matrix products, arithmetic and copies ran while one was open for 0% -> 0% of each run, Pallas kernels for 0% -> 0%
where the time goes in v4:
time: 231 us
  Pallas kernels  136 us (59%)
  waiting for transfers between devices  49.1 us (21%)
  matrix products  19.6 us (8%)
  between operations  13.5 us (6%)
  other arithmetic  12.4 us (5%)
    pallas_call x1, Pallas kernels, ring_reduce_scatter(): pl.pallas_call(functools.partial(_ring_rs_kernel, side, cols), out_shape=...  84.9 us
    pallas_call x3, Pallas kernels, exchange(): pl.pallas_call(functools.partial(_exchange_kernel, mode, axis, n, rows),...  50.6 us
    all_gather x1, waiting for transfers between devices, body(): all_hidden = lax.all_gather(hidden, 'wa', axis=0, tiled=True)  49.1 us
    dot_general x1, matrix products, body(): jnp.dot(all_hidden, down_weight, preferred_element_type=jnp.float32)  8.63 us
    dot_general x1, matrix products, body(): up_part = jnp.dot(gathered, up_weight, preferred_element_type=jnp.float32)  7.26 us
    concatenate x1, other arithmetic, body(): jnp.concatenate([gate_part, up_part], axis=1)  5.46 us
  transfers between devices with their start and end apart: 1, of which 1 were waited for; matrix products, arithmetic and copies ran while one was open for 0% of the time, Pallas kernels for 0%

profile of v4, /device:TPU:1, one launch (start us, length us, event | category | flops | bytes accessed | tf_op | source)
XLA Modules:
  0.0 230.9 jit_solution(5877303239912880617)
XLA Ops:
  6.5 0.0 all-gather.2.cloned.1.call-start
  6.5 1.0 fusion
  7.6 0.1 reshape.24
  7.6 0.6 pad.4.x_ref
  8.3 11.7 %shard_map.55 = f32[8,128]{1,0:T(8,128)} custom-call(f32[8,128]{1,0:T(8,128)} %pad.4.x_ref), custom_call_target="tpu_custom_call" | custom-call | tf_op jit(solution)/shard_map/pallas_call | solution.py:76
  20.0 0.7 add_rsqrt_fusion
  20.7 0.1 rsqrt.12
  20.7 1.7 fusion.2.x_ref
  22.4 0.0 slice-start
  22.4 20.0 %shard_map.56 = bf16[512,1024]{1,0:T(8,128)(2,1)} custom-call(bf16[64,1024]{1,0:T(8,128)(2,1)} %fusion.2.x_ref), custom_call_target="tpu_custom_call" | custom-call | tf_op jit(solution)/shard_map/pallas_call | solution.py:76
  42.4 0.0 copy-start
  42.4 0.0 slice-start.1
  42.5 7.3 %fusion.4 = f32[512,3328]{1,0:T(8,128)S(1)} fusion(bf16[512,1024]{1,0:T(8,128)(2,1)} %shard_map.56, bf16[1024,3328]{1,0:T(8,128)(2,1)} %param.8), kind=kOutput, calls=%fused_computation.10 | convolution fusion | flops 3489660928 | bytes 14680064 | tf_op jit(solution)/shard_map/dot_general | solution.py:208
  49.7 0.0 slice-done
  49.7 0.0 copy-done
  49.7 0.0 slice-done.1
  49.8 3.7 %fusion.3 = f32[512,3328]{1,0:T(8,128)S(1)} fusion(bf16[512,1024]{1,0:T(8,128)(2,1)S(1)} %copy-done, bf16[1024,3328]{1,0:T(8,128)(2,1)S(1)} %bitcast.9), kind=kOutput, calls=%fused_computation.9 | convolution fusion | flops 3489660928 | bytes 14680064 | tf_op jit(solution)/shard_map/dot_general | solution.py:207
  53.5 5.5 %pad_maximum_fusion = f32[512,6656]{1,0:T(8,128)} fusion(f32[512,3328]{1,0:T(8,128)S(1)} %fusion.4, f32[512,3328]{1,0:T(8,128)S(1)} %fusion.3), kind=kLoop, calls=%fused_computation | loop fusion | flops 3407872 | bytes 27262976 | tf_op jit(solution)/shard_map/concatenate | solution.py:209
  58.9 84.9 %shard_map.57 = f32[32,6656]{1,0:T(8,128)} custom-call(f32[4,4,32,6656]{3,2,1,0:T(8,128)} %bitcast.7), custom_call_target="tpu_custom_call" | custom-call | tf_op jit(solution)/shard_map/pallas_call | solution.py:175
  143.8 1.9 multiply_convert_fusion
  145.8 0.0 all-gather.2.cloned.1.call-update
  145.8 49.1 %all-gather.2.cloned.1.call-done = bf16[512,3328]{1,0:T(8,128)(2,1)} async-done(((bf16[32,3328]{1,0:T(8,128)(2,1)}), bf16[512,3328]{1,0:T(8,128)(2,1)}) %all-gather.2.cloned.1.call-update) | async-done | bytes 3407888 | tf_op jit(solution)/shard_map/all_gather | solution.py:213
  194.9 8.6 %convolution_convert_fusion.x_ref = bf16[512,1024]{1,0:T(8,128)(2,1)} fusion(bf16[512,3328]{1,0:T(8,128)(2,1)} %all-gather.2.cloned.1.call-done, bf16[3328,1024]{1,0:T(8,128)(2,1)} %param.9), kind=kOutput, calls=%fused_computation.1 | convolution fusion | flops 3490185216 | bytes 11272192 | tf_op jit(solution)/shard_map/dot_general | solution.py:214
  203.5 18.9 %shard_map.58 = f32[64,1024]{1,0:T(8,128)} custom-call(bf16[512,1024]{1,0:T(8,128)(2,1)} %convolution_convert_fusion.x_ref), custom_call_target="tpu_custom_call" | custom-call | tf_op jit(solution)/shard_map/pallas_call | solution.py:76
  222.4 1.6 convert_element_type.21
  (1 shorter events, 0.0 us)
Async XLA Ops:
  6.5 188.3 %all-gather.2.cloned.1.call-start = ((), (), s32[]{:S(2)}) async-start(), calls=%async_computation | async-start | bytes 3620864 | tf_op jit(solution)/shard_map/all_gather | solution.py:213
  22.4 27.3 %slice-start = ((s8[6815744]{0:T(1024)(128)(4,1)}), s8[2621440]{0:T(1024)(128)(4,1)S(1)}, s32[]{:S(2)}) async-start(s8[6815744]{0:T(1024)(128)(4,1)} %bitcast.8), calls=%async_computation.1 | async-start | bytes 5242880
  42.4 7.3 %copy-start = (bf16[512,1024]{1,0:T(8,128)(2,1)S(1)}, bf16[512,1024]{1,0:T(8,128)(2,1)}, u32[]{:S(2)}) copy-start(bf16[512,1024]{1,0:T(8,128)(2,1)} %shard_map.56) | copy-start | bytes 3145732
  42.4 7.3 %slice-start.1 = ((s8[6815744]{0:T(1024)(128)(4,1)}), s8[4194304]{0:T(1024)(128)(4,1)S(1)}, s32[]{:S(2)}) async-start(s8[6815744]{0:T(1024)(128)(4,1)} %bitcast.8), calls=%async_computation.2 | async-start | bytes 8388608
Sparse Core Ops, SparseCore 0:
  145.9 48.9 all-gather.1

commit v5 on v4

--- a/solution.py
+++ b/solution.py
@@ -191,6 +191,88 @@
     )(p4)
 
 
+def _grid_ag_kernel(side, cols, h_ref, out_ref, gath, send_sem, recv_sem, local_sem):
+    w = lax.axis_index("wa")
+    x, z = w // side, lax.rem(w, side)
+
+    def peer(axis, k):
+        if axis == 0:
+            return lax.rem(x + k, side) * side + z
+        return x * side + lax.rem(z + k, side)
+
+    barrier = pltpu.get_barrier_semaphore()
+    for axis in (0, 1):
+        for k in range(1, side):
+            pl.semaphore_signal(barrier, inc=1, device_id={"wa": peer(axis, k)}, device_id_type=MESH)
+    pl.semaphore_wait(barrier, 2 * (side - 1))
+
+    halves = [pl.ds(0, cols), pl.ds(cols, cols)]
+    locals_ = []
+    for f in range(2):
+        c = halves[f]
+        copy = pltpu.make_async_copy(h_ref.at[:, c], gath.at[x, z, :, c], local_sem.at[f])
+        copy.start()
+        locals_.append(copy)
+    sends = []
+    stage2 = []
+    stage1 = [[], []]
+    for f in range(2):
+        c = halves[f]
+        for k in range(1, side):
+            index = (f * 2 + 0) * side + k
+            copy = pltpu.make_async_remote_copy(
+                src_ref=h_ref.at[:, c], dst_ref=gath.at[x, z, :, c],
+                send_sem=send_sem.at[index], recv_sem=recv_sem.at[index],
+                device_id={"wa": peer(f, k)}, device_id_type=MESH)
+            copy.start()
+            sends.append(copy)
+            stage1[f].append(copy)
+    for f in range(2):
+        c = halves[f]
+        locals_[f].wait()
+        for copy in stage1[f]:
+            copy.wait_recv()
+        if f == 0:
+            view = gath.at[:, z, :, c]
+        else:
+            view = gath.at[x, :, :, c]
+        for k in range(1, side):
+            index = (f * 2 + 1) * side + k
+            copy = pltpu.make_async_remote_copy(
+                src_ref=view, dst_ref=view,
+                send_sem=send_sem.at[index], recv_sem=recv_sem.at[index],
+                device_id={"wa": peer(1 - f, k)}, device_id_type=MESH)
+            copy.start()
+            stage2.append(copy)
+    for copy in sends:
+        copy.wait_send()
+    for copy in stage2:
+        copy.wait()
+    final = pltpu.make_async_copy(gath, out_ref, local_sem.at[2])
+    final.start()
+    final.wait()
+
+
+def grid_all_gather(h, n, collective_id):
+    side = 4
+    rows, width = h.shape
+    cols = width // 2
+    out = pl.pallas_call(
+        functools.partial(_grid_ag_kernel, side, cols),
+        out_shape=jax.ShapeDtypeStruct((side, side, rows, width), h.dtype),
+        in_specs=[pl.BlockSpec(memory_space=pltpu.VMEM)],
+        out_specs=pl.BlockSpec(memory_space=pltpu.VMEM),
+        scratch_shapes=[
+            pltpu.VMEM((side, side, rows, width), h.dtype),
+            pltpu.SemaphoreType.DMA((4 * side,)),
+            pltpu.SemaphoreType.DMA((4 * side,)),
+            pltpu.SemaphoreType.DMA((3,)),
+        ],
+        compiler_params=pltpu.CompilerParams(collective_id=collective_id, has_side_effects=True),
+    )(h)
+    return out.reshape(n * rows, width)
+
+
 def body(tokens, norm_gain, gate_weight, up_weight, down_weight):
     n_wa = lax.axis_size("wa")
     n_ha = lax.axis_size("ha")
@@ -210,7 +292,7 @@
     gate = summed[:, :hidden_width]
     up = summed[:, hidden_width:]
     hidden = (jax.nn.silu(gate) * up).astype(jnp.bfloat16)
-    all_hidden = lax.all_gather(hidden, "wa", axis=0, tiled=True)
+    all_hidden = grid_all_gather(hidden, n_wa, 3)
     partial_out = jnp.dot(all_hidden, down_weight, preferred_element_type=jnp.float32)
     mixed_out = exchange(partial_out.astype(jnp.bfloat16), "scatter", "ha", n_ha, 4)
     return mixed_out.astype(jnp.bfloat16)

time: 231 us -> 202 us (0.87)
  waiting for transfers between devices: 49.1 us -> 0 us
  Pallas kernels: 136 us -> 169 us
  between operations: 13.5 us -> 0.11 us
    all_gather x1 -> x0, waiting for transfers between devices: 49.1 us -> none  [body(): all_hidden = lax.all_gather(hidden, 'wa', axis=0, tiled=True)]
    pallas_call x0 -> x1, Pallas kernels: none -> 29.6 us  [grid_all_gather(): pl.pallas_call(functools.partial(_grid_ag_kernel, side, cols), out_shape=...]
    pallas_call x3, Pallas kernels: 50.6 us -> 54.2 us  [exchange(): pl.pallas_call(functools.partial(_exchange_kernel, mode, axis, n, rows),...]
  transfers between devices with their start and end apart: 1 -> 0, of which waited for: 1 -> 0; matrix products, arithmetic and copies ran while one was open for 0% -> 0% of each run, Pallas kernels for 0% -> 0%
where the time goes in v5:
time: 202 us; the launch traced here: 201 us
  Pallas kernels  169 us (84%)
  matrix products  19.6 us (10%)
  other arithmetic  12.4 us (6%)
    pallas_call x1, Pallas kernels, ring_reduce_scatter(): pl.pallas_call(functools.partial(_ring_rs_kernel, side, cols), out_shape=...  84.8 us
    pallas_call x3, Pallas kernels, exchange(): pl.pallas_call(functools.partial(_exchange_kernel, mode, axis, n, rows),...  54.2 us
    pallas_call x1, Pallas kernels, grid_all_gather(): pl.pallas_call(functools.partial(_grid_ag_kernel, side, cols), out_shape=...  29.6 us
    dot_general x1, matrix products, body(): jnp.dot(all_hidden, down_weight, preferred_element_type=jnp.float32)  8.65 us
    dot_general x1, matrix products, body(): up_part = jnp.dot(gathered, up_weight, preferred_element_type=jnp.float32)  7.26 us
    concatenate x1, other arithmetic, body(): jnp.concatenate([gate_part, up_part], axis=1)  5.46 us

profile of v5, /device:TPU:1, one launch (start us, length us, event | category | flops | bytes accessed | tf_op | source)
XLA Modules:
  0.0 201.5 jit_solution(15986618026698356615)
XLA Ops:
  0.0 1.0 fusion
  1.0 0.1 reshape.27
  1.1 0.6 pad.4.x_ref
  1.7 11.7 %shard_map.55 = f32[8,128]{1,0:T(8,128)} custom-call(f32[8,128]{1,0:T(8,128)} %pad.4.x_ref), custom_call_target="tpu_custom_call" | custom-call | tf_op jit(solution)/shard_map/pallas_call | solution.py:76
  13.4 0.7 add_rsqrt_fusion
  14.1 0.1 rsqrt.12
  14.2 1.7 fusion.2.x_ref
  15.9 0.0 slice-start
  15.9 20.0 %shard_map.56 = bf16[512,1024]{1,0:T(8,128)(2,1)} custom-call(bf16[64,1024]{1,0:T(8,128)(2,1)} %fusion.2.x_ref), custom_call_target="tpu_custom_call" | custom-call | tf_op jit(solution)/shard_map/pallas_call | solution.py:76
  35.9 0.0 copy-start
  35.9 0.0 slice-start.1
  35.9 7.3 %fusion.4 = f32[512,3328]{1,0:T(8,128)S(1)} fusion(bf16[512,1024]{1,0:T(8,128)(2,1)} %shard_map.56, bf16[1024,3328]{1,0:T(8,128)(2,1)} %param.8), kind=kOutput, calls=%fused_computation.10 | convolution fusion | flops 3489660928 | bytes 14680064 | tf_op jit(solution)/shard_map/dot_general | solution.py:290
  43.2 0.0 slice-done
  43.2 0.0 copy-done
  43.2 0.0 slice-done.1
  43.2 3.7 %fusion.3 = f32[512,3328]{1,0:T(8,128)S(1)} fusion(bf16[512,1024]{1,0:T(8,128)(2,1)S(1)} %copy-done, bf16[1024,3328]{1,0:T(8,128)(2,1)S(1)} %bitcast.11), kind=kOutput, calls=%fused_computation.9 | convolution fusion | flops 3489660928 | bytes 14680064 | tf_op jit(solution)/shard_map/dot_general | solution.py:289
  46.9 5.5 %pad_maximum_fusion = f32[512,6656]{1,0:T(8,128)} fusion(f32[512,3328]{1,0:T(8,128)S(1)} %fusion.4, f32[512,3328]{1,0:T(8,128)S(1)} %fusion.3), kind=kLoop, calls=%fused_computation | loop fusion | flops 3407872 | bytes 27262976 | tf_op jit(solution)/shard_map/concatenate | solution.py:291
  52.4 84.8 %shard_map.57 = f32[32,6656]{1,0:T(8,128)} custom-call(f32[4,4,32,6656]{3,2,1,0:T(8,128)} %bitcast.8), custom_call_target="tpu_custom_call" | custom-call | tf_op jit(solution)/shard_map/pallas_call | solution.py:175
  137.1 2.0 multiply_convert_fusion.h_ref
  139.1 29.6 %shard_map.58 = bf16[4,4,32,3328]{3,2,1,0:T(8,128)(2,1)} custom-call(bf16[32,3328]{1,0:T(8,128)(2,1)} %multiply_convert_fusion.h_ref), custom_call_target="tpu_custom_call" | custom-call | tf_op jit(solution)/shard_map/pallas_call | solution.py:260
  168.7 8.7 %convolution_convert_fusion.x_ref = bf16[512,1024]{1,0:T(8,128)(2,1)} fusion(bf16[512,3328]{1,0:T(8,128)(2,1)} %bitcast.9, bf16[3328,1024]{1,0:T(8,128)(2,1)} %param.9), kind=kOutput, calls=%fused_computation.1 | convolution fusion | flops 3490185216 | bytes 11272192 | tf_op jit(solution)/shard_map/dot_general | solution.py:296
  177.4 22.5 %shard_map.59 = f32[64,1024]{1,0:T(8,128)} custom-call(bf16[512,1024]{1,0:T(8,128)(2,1)} %convolution_convert_fusion.x_ref), custom_call_target="tpu_custom_call" | custom-call | tf_op jit(solution)/shard_map/pallas_call | solution.py:76
  199.9 1.6 convert_element_type.21
  (1 shorter events, 0.0 us)
Async XLA Ops:
  15.9 27.3 %slice-start = ((s8[6815744]{0:T(1024)(128)(4,1)}), s8[2621440]{0:T(1024)(128)(4,1)S(1)}, s32[]{:S(2)}) async-start(s8[6815744]{0:T(1024)(128)(4,1)} %bitcast.10), calls=%async_computation | async-start | bytes 5242880
  35.9 7.3 %copy-start = (bf16[512,1024]{1,0:T(8,128)(2,1)S(1)}, bf16[512,1024]{1,0:T(8,128)(2,1)}, u32[]{:S(2)}) copy-start(bf16[512,1024]{1,0:T(8,128)(2,1)} %shard_map.56) | copy-start | bytes 3145732
  35.9 7.3 %slice-start.1 = ((s8[6815744]{0:T(1024)(128)(4,1)}), s8[4194304]{0:T(1024)(128)(4,1)S(1)}, s32[]{:S(2)}) async-start(s8[6815744]{0:T(1024)(128)(4,1)} %bitcast.10), calls=%async_computation.1 | async-start | bytes 8388608

commit v6 on v5

--- a/solution.py
+++ b/solution.py
@@ -87,7 +87,7 @@
     )(x)
 
 
-def _ring_rs_kernel(side, cols, p_ref, out_ref, recv1, acc1, s1, recv2, acc2, send_sem, recv_sem):
+def _ring_rs_kernel(side, cols, g_ref, u_ref, out_ref, recv1, acc1, s1, recv2, acc2, send_sem, recv_sem):
     w = lax.axis_index("wa")
     x, z = w // side, lax.rem(w, side)
 
@@ -109,7 +109,9 @@
         flows.append((first, delta, pl.ds(f * cols, cols)))
 
     def own1(f, chunk):
-        first, _, c = flows[f]
+        first = flows[f][0]
+        p_ref = g_ref if f < 2 else u_ref
+        c = pl.ds((f % 2) * cols, cols)
         if first == 0:
             return p_ref.at[chunk, :, :, c]
         return p_ref.at[:, chunk, :, c]
@@ -165,17 +167,18 @@
         copy.wait_send()
 
 
-def ring_reduce_scatter(partial, n, collective_id):
+def ring_reduce_scatter(gate_part, up_part, n, collective_id):
     side = 4
-    rows = partial.shape[0] // n
-    width = partial.shape[1]
+    rows = gate_part.shape[0] // n
+    width = 2 * gate_part.shape[1]
     cols = width // 4
-    p4 = partial.reshape(side, side, rows, width)
+    g4 = gate_part.reshape(side, side, rows, width // 2)
+    u4 = up_part.reshape(side, side, rows, width // 2)
     f32 = jnp.float32
     return pl.pallas_call(
         functools.partial(_ring_rs_kernel, side, cols),
         out_shape=jax.ShapeDtypeStruct((rows, width), f32),
-        in_specs=[pl.BlockSpec(memory_space=pltpu.VMEM)],
+        in_specs=[pl.BlockSpec(memory_space=pltpu.VMEM)] * 2,
         out_specs=pl.BlockSpec(memory_space=pltpu.VMEM),
         scratch_shapes=[
             pltpu.VMEM((4, side - 1, side, rows, cols), f32),
@@ -188,7 +191,7 @@
         ],
         compiler_params=pltpu.CompilerParams(
             collective_id=collective_id, has_side_effects=True, vmem_limit_bytes=60 * 1024 * 1024),
-    )(p4)
+    )(g4, u4)
 
 
 def _grid_ag_kernel(side, cols, h_ref, out_ref, gath, send_sem, recv_sem, local_sem):
@@ -288,7 +291,7 @@
     hidden_width = gate_weight.shape[1]
     gate_part = jnp.dot(gathered, gate_weight, preferred_element_type=jnp.float32)
     up_part = jnp.dot(gathered, up_weight, preferred_element_type=jnp.float32)
-    summed = ring_reduce_scatter(jnp.concatenate([gate_part, up_part], axis=1), n_wa, 2)
+    summed = ring_reduce_scatter(gate_part, up_part, n_wa, 2)
     gate = summed[:, :hidden_width]
     up = summed[:, hidden_width:]
     hidden = (jax.nn.silu(gate) * up).astype(jnp.bfloat16)

time: 202 us -> 201 us (level)
  other arithmetic: 12.4 us -> 6.96 us
  matrix products: 19.6 us -> 24.2 us
    concatenate x1 -> x0, other arithmetic: 5.46 us -> none  [body(): jnp.concatenate([gate_part, up_part], axis=1)]
    dot_general x1, matrix products: 7.26 us -> 9.87 us  [body(): up_part = jnp.dot(gathered, up_weight, preferred_element_type=jnp.float32)]
    dot_general x1, matrix products: 3.69 us -> 5.71 us  [body(): jnp.dot(gathered, gate_weight, preferred_element_type=jnp.float32)]
where the time goes in v6:
time: 201 us
  Pallas kernels  169 us (84%)
  matrix products  24.2 us (12%)
  other arithmetic  6.96 us (3%)
    pallas_call x1, Pallas kernels, ring_reduce_scatter(): pl.pallas_call(functools.partial(_ring_rs_kernel, side, cols), out_shape=...  84.8 us
    pallas_call x3, Pallas kernels, exchange(): pl.pallas_call(functools.partial(_exchange_kernel, mode, axis, n, rows),...  54.2 us
    pallas_call x1, Pallas kernels, grid_all_gather(): pl.pallas_call(functools.partial(_grid_ag_kernel, side, cols), out_shape=...  29.6 us
    dot_general x1, matrix products, body(): up_part = jnp.dot(gathered, up_weight, preferred_element_type=jnp.float32)  9.87 us
    dot_general x1, matrix products, body(): jnp.dot(all_hidden, down_weight, preferred_element_type=jnp.float32)  8.65 us
    dot_general x1, matrix products, body(): jnp.dot(gathered, gate_weight, preferred_element_type=jnp.float32)  5.71 us

profile of v6, /device:TPU:1, one launch (start us, length us, event | category | flops | bytes accessed | tf_op | source)
XLA Modules:
  0.0 200.7 jit_solution(4375648252125430628)
XLA Ops:
  0.0 1.0 fusion
  1.0 0.1 reshape.30
  1.1 0.6 pad.4.x_ref
  1.7 11.7 %shard_map.55 = f32[8,128]{1,0:T(8,128)} custom-call(f32[8,128]{1,0:T(8,128)} %pad.4.x_ref), custom_call_target="tpu_custom_call" | custom-call | tf_op jit(solution)/shard_map/pallas_call | solution.py:76
  13.4 0.7 add_rsqrt_fusion
  14.1 0.1 rsqrt.12
  14.2 1.7 fusion.2.x_ref
  15.9 0.0 slice-start
  15.9 20.0 %shard_map.56 = bf16[512,1024]{1,0:T(8,128)(2,1)} custom-call(bf16[64,1024]{1,0:T(8,128)(2,1)} %fusion.2.x_ref), custom_call_target="tpu_custom_call" | custom-call | tf_op jit(solution)/shard_map/pallas_call | solution.py:76
  35.9 0.0 copy-start
  35.9 0.0 slice-start.1
  35.9 9.9 %fusion.4 = f32[512,3328]{1,0:T(8,128)} fusion(bf16[512,1024]{1,0:T(8,128)(2,1)} %shard_map.56, bf16[1024,3328]{1,0:T(8,128)(2,1)} %param.8), kind=kOutput, calls=%fused_computation.9 | convolution fusion | flops 3489660928 | bytes 14680064 | tf_op jit(solution)/shard_map/dot_general | solution.py:293
  45.8 0.0 slice-done
  45.8 0.0 copy-done
  45.8 0.0 slice-done.1
  45.8 5.7 %fusion.3 = f32[512,3328]{1,0:T(8,128)} fusion(bf16[512,1024]{1,0:T(8,128)(2,1)S(1)} %copy-done, bf16[1024,3328]{1,0:T(8,128)(2,1)S(1)} %bitcast.13), kind=kOutput, calls=%fused_computation.8 | convolution fusion | flops 3489660928 | bytes 14680064 | tf_op jit(solution)/shard_map/dot_general | solution.py:292
  51.5 84.8 %shard_map.57 = f32[32,6656]{1,0:T(8,128)} custom-call(f32[4,4,32,3328]{3,2,1,0:T(8,128)} %bitcast.10, f32[4,4,32,3328]{3,2,1,0:T(8,128)} %bitcast.9), custom_call_target="tpu_custom_call" | custom-call | tf_op jit(solution)/shard_map/pallas_call | solution.py:178
  136.3 2.0 multiply_convert_fusion.h_ref
  138.2 29.6 %shard_map.58 = bf16[4,4,32,3328]{3,2,1,0:T(8,128)(2,1)} custom-call(bf16[32,3328]{1,0:T(8,128)(2,1)} %multiply_convert_fusion.h_ref), custom_call_target="tpu_custom_call" | custom-call | tf_op jit(solution)/shard_map/pallas_call | solution.py:263
  167.8 8.7 %convolution_convert_fusion.x_ref = bf16[512,1024]{1,0:T(8,128)(2,1)} fusion(bf16[512,3328]{1,0:T(8,128)(2,1)} %bitcast.11, bf16[3328,1024]{1,0:T(8,128)(2,1)} %param.9), kind=kOutput, calls=%fused_computation | convolution fusion | flops 3490185216 | bytes 11272192 | tf_op jit(solution)/shard_map/dot_general | solution.py:299
  176.5 22.5 %shard_map.59 = f32[64,1024]{1,0:T(8,128)} custom-call(bf16[512,1024]{1,0:T(8,128)(2,1)} %convolution_convert_fusion.x_ref), custom_call_target="tpu_custom_call" | custom-call | tf_op jit(solution)/shard_map/pallas_call | solution.py:76
  199.0 1.6 convert_element_type.21
  (1 shorter events, 0.0 us)
Async XLA Ops:
  15.9 29.9 %slice-start = ((s8[6815744]{0:T(1024)(128)(4,1)}), s8[2621440]{0:T(1024)(128)(4,1)S(1)}, s32[]{:S(2)}) async-start(s8[6815744]{0:T(1024)(128)(4,1)} %bitcast.12), calls=%async_computation | async-start | bytes 5242880
  35.9 9.9 %copy-start = (bf16[512,1024]{1,0:T(8,128)(2,1)S(1)}, bf16[512,1024]{1,0:T(8,128)(2,1)}, u32[]{:S(2)}) copy-start(bf16[512,1024]{1,0:T(8,128)(2,1)} %shard_map.56) | copy-start | bytes 3145732
  35.9 9.9 %slice-start.1 = ((s8[6815744]{0:T(1024)(128)(4,1)}), s8[4194304]{0:T(1024)(128)(4,1)S(1)}, s32[]{:S(2)}) async-start(s8[6815744]{0:T(1024)(128)(4,1)} %bitcast.12), calls=%async_computation.1 | async-start | bytes 8388608

commit v7 on v5

--- a/solution.py
+++ b/solution.py
@@ -87,9 +87,16 @@
     )(x)
 
 
-def _ring_rs_kernel(side, cols, p_ref, out_ref, recv1, acc1, s1, recv2, acc2, send_sem, recv_sem):
+def _ring_rs_kernel(side, cols, t_ref, g_hbm, u_hbm, out_ref, wbuf, first_buf, tmp, recv1, acc1, s1,
+                    recv2, acc2, send_sem, recv_sem, w_sem):
     w = lax.axis_index("wa")
     x, z = w // side, lax.rem(w, side)
+    loads = []
+    for f in range(4):
+        source = g_hbm if f < 2 else u_hbm
+        load = pltpu.make_async_copy(source.at[:, pl.ds((f % 2) * cols, cols)], wbuf.at[f], w_sem.at[f])
+        load.start()
+        loads.append(load)
 
     def peer(axis, delta):
         if axis == 0:
@@ -109,10 +116,13 @@
         flows.append((first, delta, pl.ds(f * cols, cols)))
 
     def own1(f, chunk):
-        first, _, c = flows[f]
-        if first == 0:
-            return p_ref.at[chunk, :, :, c]
-        return p_ref.at[:, chunk, :, c]
+        if flows[f][0] == 0:
+            rows = t_ref[chunk]
+        else:
+            rows = t_ref[:, chunk]
+        block = rows.reshape(side * rows.shape[1], rows.shape[2])
+        product = jnp.dot(block, wbuf[f], preferred_element_type=jnp.float32)
+        return product.reshape(side, rows.shape[1], cols)
 
     def sem(stage, step, f):
         return (stage * 3 + step) * 4 + f
@@ -126,10 +136,13 @@
             first, delta, _ = flows[f]
             chunk = lax.rem(pos1[f] - delta * (step + 1) + 2 * side, side)
             if step == 0:
-                source = own1(f, chunk)
+                loads[f].wait()
+                first_buf[f] = own1(f, chunk)
+                source = first_buf.at[f]
             else:
+                tmp[f] = own1(f, chunk)
                 last[f].wait_recv()
-                acc1[f, step - 1] = recv1[f, step - 1] + own1(f, chunk)[...]
+                acc1[f, step - 1] = recv1[f, step - 1] + tmp[f]
                 source = acc1.at[f, step - 1]
             copy = pltpu.make_async_remote_copy(
                 src_ref=source, dst_ref=recv1.at[f, step],
@@ -139,8 +152,9 @@
             sends.append(copy)
             last[f] = copy
     for f in range(4):
+        tmp[f] = own1(f, pos1[f])
         last[f].wait_recv()
-        s1[f] = recv1[f, side - 2] + own1(f, pos1[f])[...]
+        s1[f] = recv1[f, side - 2] + tmp[f]
     for step in range(side - 1):
         for f in range(4):
             first, delta, _ = flows[f]
@@ -165,19 +179,24 @@
         copy.wait_send()
 
 
-def ring_reduce_scatter(partial, n, collective_id):
+def ring_reduce_scatter(tokens, gate_weight, up_weight, n, collective_id):
     side = 4
-    rows = partial.shape[0] // n
-    width = partial.shape[1]
+    rows = tokens.shape[0] // n
+    depth = tokens.shape[1]
+    width = 2 * gate_weight.shape[1]
     cols = width // 4
-    p4 = partial.reshape(side, side, rows, width)
+    t4 = tokens.reshape(side, side, rows, depth)
     f32 = jnp.float32
     return pl.pallas_call(
         functools.partial(_ring_rs_kernel, side, cols),
         out_shape=jax.ShapeDtypeStruct((rows, width), f32),
-        in_specs=[pl.BlockSpec(memory_space=pltpu.VMEM)],
+        in_specs=[pl.BlockSpec(memory_space=pltpu.VMEM), pl.BlockSpec(memory_space=pl.ANY),
+                  pl.BlockSpec(memory_space=pl.ANY)],
         out_specs=pl.BlockSpec(memory_space=pltpu.VMEM),
         scratch_shapes=[
+            pltpu.VMEM((4, depth, cols), gate_weight.dtype),
+            pltpu.VMEM((4, side, rows, cols), f32),
+            pltpu.VMEM((4, side, rows, cols), f32),
             pltpu.VMEM((4, side - 1, side, rows, cols), f32),
             pltpu.VMEM((4, side - 2, side, rows, cols), f32),
             pltpu.VMEM((4, side, rows, cols), f32),
@@ -185,10 +204,11 @@
             pltpu.VMEM((4, side - 2, rows, cols), f32),
             pltpu.SemaphoreType.DMA((24,)),
             pltpu.SemaphoreType.DMA((24,)),
+            pltpu.SemaphoreType.DMA((4,)),
         ],
         compiler_params=pltpu.CompilerParams(
-            collective_id=collective_id, has_side_effects=True, vmem_limit_bytes=60 * 1024 * 1024),
-    )(p4)
+            collective_id=collective_id, has_side_effects=True, vmem_limit_bytes=63 * 1024 * 1024),
+    )(t4, gate_weight, up_weight)
 
 
 def _grid_ag_kernel(side, cols, h_ref, out_ref, gath, send_sem, recv_sem, local_sem):
@@ -286,9 +306,7 @@
     normed = (own_values * lax.rsqrt(mean_square + 1e-05) * norm_gain[None, :]).astype(jnp.bfloat16)
     gathered = exchange(normed, "gather", "ha", n_ha, 1)
     hidden_width = gate_weight.shape[1]
-    gate_part = jnp.dot(gathered, gate_weight, preferred_element_type=jnp.float32)
-    up_part = jnp.dot(gathered, up_weight, preferred_element_type=jnp.float32)
-    summed = ring_reduce_scatter(jnp.concatenate([gate_part, up_part], axis=1), n_wa, 2)
+    summed = ring_reduce_scatter(gathered, gate_weight, up_weight, n_wa, 2)
     gate = summed[:, :hidden_width]
     up = summed[:, hidden_width:]
     hidden = (jax.nn.silu(gate) * up).astype(jnp.bfloat16)

time: 202 us -> 186 us (0.921)
  matrix products: 19.6 us -> 8.65 us
  other arithmetic: 12.4 us -> 6.95 us
    dot_general x2 -> x0, matrix products: 10.9 us -> none  [the longest x1 7.26 us: body(): up_part = jnp.dot(gathered, up_weight, preferred_element_type=jnp.float32)]
    concatenate x1 -> x0, other arithmetic: 5.46 us -> none  [body(): jnp.concatenate([gate_part, up_part], axis=1)]
where the time goes in v7:
time: 186 us; the launch traced here: 185 us
  Pallas kernels  169 us (91%)
  matrix products  8.65 us (5%)
  other arithmetic  6.95 us (4%)
    pallas_call x1, Pallas kernels, ring_reduce_scatter(): pl.pallas_call(functools.partial(_ring_rs_kernel, side, cols), out_shape=...  85.7 us
    pallas_call x3, Pallas kernels, exchange(): pl.pallas_call(functools.partial(_exchange_kernel, mode, axis, n, rows),...  53.9 us
    pallas_call x1, Pallas kernels, grid_all_gather(): pl.pallas_call(functools.partial(_grid_ag_kernel, side, cols), out_shape=...  29.2 us
    dot_general x1, matrix products, body(): jnp.dot(all_hidden, down_weight, preferred_element_type=jnp.float32)  8.65 us

profile of v7, /device:TPU:1, one launch (start us, length us, event | category | flops | bytes accessed | tf_op | source)
XLA Modules:
  0.0 185.2 jit_solution(1439186918063342073)
XLA Ops:
  0.0 1.0 fusion
  1.0 0.1 reshape.27
  1.1 0.6 pad.4.x_ref
  1.7 11.7 %shard_map.55 = f32[8,128]{1,0:T(8,128)} custom-call(f32[8,128]{1,0:T(8,128)} %pad.4.x_ref), custom_call_target="tpu_custom_call" | custom-call | tf_op jit(solution)/shard_map/pallas_call | solution.py:76
  13.4 0.7 add_rsqrt_fusion
  14.1 0.1 rsqrt.12
  14.2 1.7 fusion.2.x_ref
  15.9 19.9 %shard_map.56 = bf16[512,1024]{1,0:T(8,128)(2,1)} custom-call(bf16[64,1024]{1,0:T(8,128)(2,1)} %fusion.2.x_ref), custom_call_target="tpu_custom_call" | custom-call | tf_op jit(solution)/shard_map/pallas_call | solution.py:76
  35.8 85.7 %shard_map.57 = f32[32,6656]{1,0:T(8,128)} custom-call(bf16[4,4,32,1024]{3,2,1,0:T(8,128)(2,1)} %bitcast.4, bf16[1024,3328]{1,0:T(8,128)(2,1)} %g_hbm.1, bf16[1024,3328]{1,0:T(8,128)(2,1)} %u_hbm.1), custom_call_target="tpu_custom_call" | custom-call | tf_op jit(solution)/shard_map/pallas_call | solution.py:190
  121.5 1.9 %multiply_convert_fusion.h_ref = bf16[32,3328]{1,0:T(8,128)(2,1)} fusion(f32[32,6656]{1,0:T(8,128)} %shard_map.57), kind=kLoop, calls=%fused_computation.1 | loop fusion | flops 638976 | bytes 1064960 | tf_op jit(solution)/shard_map/convert_element_type | solution.py:312
  123.4 29.2 %shard_map.58 = bf16[4,4,32,3328]{3,2,1,0:T(8,128)(2,1)} custom-call(bf16[32,3328]{1,0:T(8,128)(2,1)} %multiply_convert_fusion.h_ref), custom_call_target="tpu_custom_call" | custom-call | tf_op jit(solution)/shard_map/pallas_call | solution.py:280
  152.6 8.7 %convolution_convert_fusion.x_ref = bf16[512,1024]{1,0:T(8,128)(2,1)} fusion(bf16[512,3328]{1,0:T(8,128)(2,1)} %bitcast.5, bf16[3328,1024]{1,0:T(8,128)(2,1)} %param.9), kind=kOutput, calls=%fused_computation | convolution fusion | flops 3490185216 | bytes 11272192 | tf_op jit(solution)/shard_map/dot_general | solution.py:314
  161.3 22.3 %shard_map.59 = f32[64,1024]{1,0:T(8,128)} custom-call(bf16[512,1024]{1,0:T(8,128)(2,1)} %convolution_convert_fusion.x_ref), custom_call_target="tpu_custom_call" | custom-call | tf_op jit(solution)/shard_map/pallas_call | solution.py:76
  183.6 1.6 convert_element_type.21

commit v8 on v7

--- a/solution.py
+++ b/solution.py
@@ -293,6 +293,52 @@
     return out.reshape(n * rows, width)
 
 
+def _down_rs_kernel(n, rows, h_ref, w_hbm, out_ref, wbuf, sendbuf, slots, send_sem, recv_sem, w_sem):
+    me = lax.axis_index("ha")
+    load = pltpu.make_async_copy(w_hbm, wbuf, w_sem.at[0])
+    load.start()
+    _greet("ha", n, me)
+    load.wait()
+    copies = []
+    for k in range(1, n):
+        peer = lax.rem(me + k, n)
+        block = h_ref[pl.ds(pl.multiple_of(peer * rows, rows), rows), :]
+        sendbuf[k] = jnp.dot(block, wbuf[...], preferred_element_type=jnp.float32).astype(sendbuf.dtype)
+        copy = pltpu.make_async_remote_copy(
+            src_ref=sendbuf.at[k], dst_ref=slots.at[k],
+            send_sem=send_sem.at[k], recv_sem=recv_sem.at[k],
+            device_id={"ha": peer}, device_id_type=MESH)
+        copy.start()
+        copies.append(copy)
+    block = h_ref[pl.ds(pl.multiple_of(me * rows, rows), rows), :]
+    total = jnp.dot(block, wbuf[...], preferred_element_type=jnp.float32)
+    for k, copy in enumerate(copies, 1):
+        copy.wait()
+        total = total + slots[k].astype(jnp.float32)
+    out_ref[...] = total
+
+
+def down_reduce_scatter(hidden, down_weight, n, collective_id):
+    rows = hidden.shape[0] // n
+    depth, width = down_weight.shape
+    return pl.pallas_call(
+        functools.partial(_down_rs_kernel, n, rows),
+        out_shape=jax.ShapeDtypeStruct((rows, width), jnp.float32),
+        in_specs=[pl.BlockSpec(memory_space=pltpu.VMEM), pl.BlockSpec(memory_space=pl.ANY)],
+        out_specs=pl.BlockSpec(memory_space=pltpu.VMEM),
+        scratch_shapes=[
+            pltpu.VMEM((depth, width), down_weight.dtype),
+            pltpu.VMEM((n, rows, width), jnp.bfloat16),
+            pltpu.VMEM((n, rows, width), jnp.bfloat16),
+            pltpu.SemaphoreType.DMA((n,)),
+            pltpu.SemaphoreType.DMA((n,)),
+            pltpu.SemaphoreType.DMA((1,)),
+        ],
+        compiler_params=pltpu.CompilerParams(
+            collective_id=collective_id, has_side_effects=True, vmem_limit_bytes=48 * 1024 * 1024),
+    )(hidden, down_weight)
+
+
 def body(tokens, norm_gain, gate_weight, up_weight, down_weight):
     n_wa = lax.axis_size("wa")
     n_ha = lax.axis_size("ha")
@@ -311,8 +357,7 @@
     up = summed[:, hidden_width:]
     hidden = (jax.nn.silu(gate) * up).astype(jnp.bfloat16)
     all_hidden = grid_all_gather(hidden, n_wa, 3)
-    partial_out = jnp.dot(all_hidden, down_weight, preferred_element_type=jnp.float32)
-    mixed_out = exchange(partial_out.astype(jnp.bfloat16), "scatter", "ha", n_ha, 4)
+    mixed_out = down_reduce_scatter(all_hidden, down_weight, n_ha, 4)
     return mixed_out.astype(jnp.bfloat16)
 
 

time: 186 us -> 178 us (0.957)
  matrix products: 8.65 us -> 0 us
  local copies, waits for them, and re-layouts: 0.77 us -> 2.73 us
    pallas_call x0 -> x1, Pallas kernels: none -> 22.7 us  [down_reduce_scatter(): pl.pallas_call(functools.partial(_down_rs_kernel, n, rows), out_shape=jax...]
    pallas_call x3 -> x2, Pallas kernels: 53.9 us -> 31.6 us  [exchange(): pl.pallas_call(functools.partial(_exchange_kernel, mode, axis, n, rows),...]
    dot_general x1 -> x0, matrix products: 8.65 us -> none  [body(): jnp.dot(all_hidden, down_weight, preferred_element_type=jnp.float32)]
    unnamed x0 -> x2, local copies, waits for them, and re-layouts: none -> 1.96 us
where the time goes in v8:
time: 178 us
  Pallas kernels  169 us (95%)
  other arithmetic  6 us (3%)
  local copies, waits for them, and re-layouts  2.73 us (2%)
    pallas_call x1, Pallas kernels, ring_reduce_scatter(): pl.pallas_call(functools.partial(_ring_rs_kernel, side, cols), out_shape=...  85.7 us
    pallas_call x2, Pallas kernels, exchange(): pl.pallas_call(functools.partial(_exchange_kernel, mode, axis, n, rows),...  31.6 us
    pallas_call x1, Pallas kernels, grid_all_gather(): pl.pallas_call(functools.partial(_grid_ag_kernel, side, cols), out_shape=...  29.2 us
    pallas_call x1, Pallas kernels, down_reduce_scatter(): pl.pallas_call(functools.partial(_down_rs_kernel, n, rows), out_shape=jax...  22.7 us

profile of v8, /device:TPU:1, one launch (start us, length us, event | category | flops | bytes accessed | tf_op | source)
XLA Modules:
  0.0 178.0 jit_solution(4741286222167837507)
XLA Ops:
  0.0 1.0 fusion
  1.0 0.1 reshape.27
  1.1 0.6 pad.4.x_ref
  1.7 11.7 %shard_map.55 = f32[8,128]{1,0:T(8,128)} custom-call(f32[8,128]{1,0:T(8,128)} %pad.4.x_ref), custom_call_target="tpu_custom_call" | custom-call | tf_op jit(solution)/shard_map/pallas_call | solution.py:76
  13.4 0.7 add_rsqrt_fusion
  14.1 0.1 rsqrt.12
  14.2 1.7 fusion.2.x_ref
  15.9 19.9 %shard_map.56 = bf16[512,1024]{1,0:T(8,128)(2,1)} custom-call(bf16[64,1024]{1,0:T(8,128)(2,1)} %fusion.2.x_ref), custom_call_target="tpu_custom_call" | custom-call | tf_op jit(solution)/shard_map/pallas_call | solution.py:76
  35.8 85.7 %shard_map.57 = f32[32,6656]{1,0:T(8,128)} custom-call(bf16[4,4,32,1024]{3,2,1,0:T(8,128)(2,1)} %bitcast.3, bf16[1024,3328]{1,0:T(8,128)(2,1)} %g_hbm.1, bf16[1024,3328]{1,0:T(8,128)(2,1)} %u_hbm.1), custom_call_target="tpu_custom_call" | custom-call | tf_op jit(solution)/shard_map/pallas_call | solution.py:190
  121.5 1.9 %multiply_convert_fusion.h_ref = bf16[32,3328]{1,0:T(8,128)(2,1)} fusion(f32[32,6656]{1,0:T(8,128)} %shard_map.57), kind=kLoop, calls=%fused_computation | loop fusion | flops 638976 | bytes 1064960 | tf_op jit(solution)/shard_map/convert_element_type | solution.py:358
  123.4 29.2 %shard_map.58 = bf16[4,4,32,3328]{3,2,1,0:T(8,128)(2,1)} custom-call(bf16[32,3328]{1,0:T(8,128)(2,1)} %multiply_convert_fusion.h_ref), custom_call_target="tpu_custom_call" | custom-call | tf_op jit(solution)/shard_map/pallas_call | solution.py:280
  152.6 0.0 copy-start
  152.6 2.0 %copy-done = bf16[4,4,32,3328]{3,2,1,0:T(8,128)(2,1)S(1)} copy-done((bf16[4,4,32,3328]{3,2,1,0:T(8,128)(2,1)S(1)}, bf16[4,4,32,3328]{3,2,1,0:T(8,128)(2,1)}, u32[]{:S(2)}) %copy-start) | copy-done | bytes 3407896
  154.6 22.7 %shard_map.59 = f32[64,1024]{1,0:T(8,128)S(1)} custom-call(bf16[512,3328]{1,0:T(8,128)(2,1)S(1)} %bitcast.2, bf16[3328,1024]{1,0:T(8,128)(2,1)} %w_hbm.1), custom_call_target="tpu_custom_call" | custom-call | tf_op jit(solution)/shard_map/pallas_call | solution.py:324
  177.3 0.7 convert_element_type.17
Async XLA Ops:
  152.6 2.0 %copy-start = (bf16[4,4,32,3328]{3,2,1,0:T(8,128)(2,1)S(1)}, bf16[4,4,32,3328]{3,2,1,0:T(8,128)(2,1)}, u32[]{:S(2)}) copy-start(bf16[4,4,32,3328]{3,2,1,0:T(8,128)(2,1)} %shard_map.58) | copy-start | bytes 10223620

commit v9 on v8

--- a/solution.py
+++ b/solution.py
@@ -87,7 +87,7 @@
     )(x)
 
 
-def _ring_rs_kernel(side, cols, t_ref, g_hbm, u_hbm, out_ref, wbuf, first_buf, tmp, recv1, acc1, s1,
+def _ring_rs_kernel(side, cols, parts, t_ref, g_hbm, u_hbm, out_ref, wbuf, first_buf, tmp, recv1, acc1, s1,
                     recv2, acc2, send_sem, recv_sem, w_sem):
     w = lax.axis_index("wa")
     x, z = w // side, lax.rem(w, side)
@@ -124,13 +124,25 @@
         product = jnp.dot(block, wbuf[f], preferred_element_type=jnp.float32)
         return product.reshape(side, rows.shape[1], cols)
 
-    def sem(stage, step, f):
-        return (stage * 3 + step) * 4 + f
-
+    def sem(stage, step, f, h):
+        return ((stage * 3 + step) * 4 + f) * parts + h
+
+    sub = t_ref.shape[2] // parts
+    halves = [pl.ds(h * sub, sub) for h in range(parts)]
     sends = []
     pos1 = [x if flows[f][0] == 0 else z for f in range(4)]
     pos2 = [z if flows[f][0] == 0 else x for f in range(4)]
-    last = [None] * 4
+    last = [[None] * parts for _ in range(4)]
+
+    def send(stage, step, f, h, source, target, axis):
+        copy = pltpu.make_async_remote_copy(
+            src_ref=source, dst_ref=target,
+            send_sem=send_sem.at[sem(stage, step, f, h)], recv_sem=recv_sem.at[sem(stage, step, f, h)],
+            device_id={"wa": peer(axis, flows[f][1])}, device_id_type=MESH)
+        copy.start()
+        sends.append(copy)
+        last[f][h] = copy
+
     for step in range(side - 1):
         for f in range(4):
             first, delta, _ = flows[f]
@@ -138,43 +150,34 @@
             if step == 0:
                 loads[f].wait()
                 first_buf[f] = own1(f, chunk)
-                source = first_buf.at[f]
+                for h, r in enumerate(halves):
+                    send(0, step, f, h, first_buf.at[f, :, r], recv1.at[f, step, :, r], first)
             else:
                 tmp[f] = own1(f, chunk)
-                last[f].wait_recv()
-                acc1[f, step - 1] = recv1[f, step - 1] + tmp[f]
-                source = acc1.at[f, step - 1]
-            copy = pltpu.make_async_remote_copy(
-                src_ref=source, dst_ref=recv1.at[f, step],
-                send_sem=send_sem.at[sem(0, step, f)], recv_sem=recv_sem.at[sem(0, step, f)],
-                device_id={"wa": peer(first, delta)}, device_id_type=MESH)
-            copy.start()
-            sends.append(copy)
-            last[f] = copy
+                for h, r in enumerate(halves):
+                    last[f][h].wait_recv()
+                    acc1[f, step - 1, :, r] = recv1[f, step - 1, :, r] + tmp[f, :, r]
+                    send(0, step, f, h, acc1.at[f, step - 1, :, r], recv1.at[f, step, :, r], first)
     for f in range(4):
+        first, delta, _ = flows[f]
         tmp[f] = own1(f, pos1[f])
-        last[f].wait_recv()
-        s1[f] = recv1[f, side - 2] + tmp[f]
-    for step in range(side - 1):
+        chunk = lax.rem(pos2[f] - delta + 2 * side, side)
+        for h, r in enumerate(halves):
+            last[f][h].wait_recv()
+            s1[f, :, r] = recv1[f, side - 2, :, r] + tmp[f, :, r]
+            send(1, 0, f, h, s1.at[f, chunk, r], recv2.at[f, 0, r], 1 - first)
+    for step in range(1, side - 1):
         for f in range(4):
             first, delta, _ = flows[f]
             chunk = lax.rem(pos2[f] - delta * (step + 1) + 2 * side, side)
-            if step == 0:
-                source = s1.at[f, chunk]
-            else:
-                last[f].wait_recv()
-                acc2[f, step - 1] = recv2[f, step - 1] + s1[f, chunk]
-                source = acc2.at[f, step - 1]
-            copy = pltpu.make_async_remote_copy(
-                src_ref=source, dst_ref=recv2.at[f, step],
-                send_sem=send_sem.at[sem(1, step, f)], recv_sem=recv_sem.at[sem(1, step, f)],
-                device_id={"wa": peer(1 - first, delta)}, device_id_type=MESH)
-            copy.start()
-            sends.append(copy)
-            last[f] = copy
+            for h, r in enumerate(halves):
+                last[f][h].wait_recv()
+                acc2[f, step - 1, r] = recv2[f, step - 1, r] + s1[f, chunk, r]
+                send(1, step, f, h, acc2.at[f, step - 1, r], recv2.at[f, step, r], 1 - first)
     for f in range(4):
-        last[f].wait_recv()
-        out_ref[:, flows[f][2]] = recv2[f, side - 2] + s1[f, pos2[f]]
+        for h, r in enumerate(halves):
+            last[f][h].wait_recv()
+            out_ref[r, flows[f][2]] = recv2[f, side - 2, r] + s1[f, pos2[f], r]
     for copy in sends:
         copy.wait_send()
 
@@ -188,7 +191,7 @@
     t4 = tokens.reshape(side, side, rows, depth)
     f32 = jnp.float32
     return pl.pallas_call(
-        functools.partial(_ring_rs_kernel, side, cols),
+        functools.partial(_ring_rs_kernel, side, cols, 2),
         out_shape=jax.ShapeDtypeStruct((rows, width), f32),
         in_specs=[pl.BlockSpec(memory_space=pltpu.VMEM), pl.BlockSpec(memory_space=pl.ANY),
                   pl.BlockSpec(memory_space=pl.ANY)],
@@ -202,8 +205,8 @@
             pltpu.VMEM((4, side, rows, cols), f32),
             pltpu.VMEM((4, side - 1, rows, cols), f32),
             pltpu.VMEM((4, side - 2, rows, cols), f32),
-            pltpu.SemaphoreType.DMA((24,)),
-            pltpu.SemaphoreType.DMA((24,)),
+            pltpu.SemaphoreType.DMA((48,)),
+            pltpu.SemaphoreType.DMA((48,)),
             pltpu.SemaphoreType.DMA((4,)),
         ],
         compiler_params=pltpu.CompilerParams(

time: 178 us -> 178 us (level)
    pallas_call x1, Pallas kernels: 29.2 us -> 31.2 us  [grid_all_gather(): pl.pallas_call(functools.partial(_grid_ag_kernel, side, cols), out_shape=...]
    pallas_call x1, Pallas kernels: 22.7 us -> 20.8 us  [down_reduce_scatter(): pl.pallas_call(functools.partial(_down_rs_kernel, n, rows), out_shape=jax...]
where the time goes in v9:
time: 178 us
  Pallas kernels  169 us (95%)
  other arithmetic  6 us (3%)
  local copies, waits for them, and re-layouts  2.73 us (2%)
    pallas_call x1, Pallas kernels, ring_reduce_scatter(): pl.pallas_call(functools.partial(_ring_rs_kernel, side, cols, 2), out_sha...  85.5 us
    pallas_call x2, Pallas kernels, exchange(): pl.pallas_call(functools.partial(_exchange_kernel, mode, axis, n, rows),...  31.6 us
    pallas_call x1, Pallas kernels, grid_all_gather(): pl.pallas_call(functools.partial(_grid_ag_kernel, side, cols), out_shape=...  31.2 us
    pallas_call x1, Pallas kernels, down_reduce_scatter(): pl.pallas_call(functools.partial(_down_rs_kernel, n, rows), out_shape=jax...  20.8 us

profile of v9, /device:TPU:1, one launch (start us, length us, event | category | flops | bytes accessed | tf_op | source)
XLA Modules:
  0.0 177.9 jit_solution(13478132591812060338)
XLA Ops:
  0.0 1.0 fusion
  1.0 0.1 reshape.27
  1.1 0.6 pad.4.x_ref
  1.7 11.7 %shard_map.55 = f32[8,128]{1,0:T(8,128)} custom-call(f32[8,128]{1,0:T(8,128)} %pad.4.x_ref), custom_call_target="tpu_custom_call" | custom-call | tf_op jit(solution)/shard_map/pallas_call | solution.py:76
  13.4 0.7 add_rsqrt_fusion
  14.1 0.1 rsqrt.12
  14.2 1.7 fusion.2.x_ref
  15.9 19.9 %shard_map.56 = bf16[512,1024]{1,0:T(8,128)(2,1)} custom-call(bf16[64,1024]{1,0:T(8,128)(2,1)} %fusion.2.x_ref), custom_call_target="tpu_custom_call" | custom-call | tf_op jit(solution)/shard_map/pallas_call | solution.py:76
  35.8 85.5 %shard_map.57 = f32[32,6656]{1,0:T(8,128)} custom-call(bf16[4,4,32,1024]{3,2,1,0:T(8,128)(2,1)} %bitcast.3, bf16[1024,3328]{1,0:T(8,128)(2,1)} %g_hbm.1, bf16[1024,3328]{1,0:T(8,128)(2,1)} %u_hbm.1), custom_call_target="tpu_custom_call" | custom-call | tf_op jit(solution)/shard_map/pallas_call | solution.py:193
  121.3 1.9 %multiply_convert_fusion.h_ref = bf16[32,3328]{1,0:T(8,128)(2,1)} fusion(f32[32,6656]{1,0:T(8,128)} %shard_map.57), kind=kLoop, calls=%fused_computation | loop fusion | flops 638976 | bytes 1064960 | tf_op jit(solution)/shard_map/convert_element_type | solution.py:361
  123.2 31.2 %shard_map.58 = bf16[4,4,32,3328]{3,2,1,0:T(8,128)(2,1)} custom-call(bf16[32,3328]{1,0:T(8,128)(2,1)} %multiply_convert_fusion.h_ref), custom_call_target="tpu_custom_call" | custom-call | tf_op jit(solution)/shard_map/pallas_call | solution.py:283
  154.5 0.0 copy-start
  154.5 2.0 %copy-done = bf16[4,4,32,3328]{3,2,1,0:T(8,128)(2,1)S(1)} copy-done((bf16[4,4,32,3328]{3,2,1,0:T(8,128)(2,1)S(1)}, bf16[4,4,32,3328]{3,2,1,0:T(8,128)(2,1)}, u32[]{:S(2)}) %copy-start) | copy-done | bytes 3407896
  156.4 20.8 %shard_map.59 = f32[64,1024]{1,0:T(8,128)S(1)} custom-call(bf16[512,3328]{1,0:T(8,128)(2,1)S(1)} %bitcast.2, bf16[3328,1024]{1,0:T(8,128)(2,1)} %w_hbm.1), custom_call_target="tpu_custom_call" | custom-call | tf_op jit(solution)/shard_map/pallas_call | solution.py:327
  177.2 0.7 convert_element_type.17
Async XLA Ops:
  154.5 2.0 %copy-start = (bf16[4,4,32,3328]{3,2,1,0:T(8,128)(2,1)S(1)}, bf16[4,4,32,3328]{3,2,1,0:T(8,128)(2,1)}, u32[]{:S(2)}) copy-start(bf16[4,4,32,3328]{3,2,1,0:T(8,128)(2,1)} %shard_map.58) | copy-start | bytes 10223620

commit v10 on v9

--- a/solution.py
+++ b/solution.py
@@ -218,59 +218,78 @@
     w = lax.axis_index("wa")
     x, z = w // side, lax.rem(w, side)
 
-    def peer(axis, k):
+    def peer(axis, delta):
         if axis == 0:
-            return lax.rem(x + k, side) * side + z
-        return x * side + lax.rem(z + k, side)
+            return lax.rem(x + delta + side, side) * side + z
+        return x * side + lax.rem(z + delta + side, side)
 
     barrier = pltpu.get_barrier_semaphore()
     for axis in (0, 1):
-        for k in range(1, side):
-            pl.semaphore_signal(barrier, inc=1, device_id={"wa": peer(axis, k)}, device_id_type=MESH)
-    pl.semaphore_wait(barrier, 2 * (side - 1))
+        for delta in (1, -1):
+            pl.semaphore_signal(barrier, inc=1, device_id={"wa": peer(axis, delta)}, device_id_type=MESH)
+    pl.semaphore_wait(barrier, 4)
 
     halves = [pl.ds(0, cols), pl.ds(cols, cols)]
+    rows = h_ref.shape[0]
     locals_ = []
     for f in range(2):
         c = halves[f]
         copy = pltpu.make_async_copy(h_ref.at[:, c], gath.at[x, z, :, c], local_sem.at[f])
         copy.start()
         locals_.append(copy)
+
+    def piece(f, stage, at, part=None):
+        c = halves[f]
+        along_x = (f == 0) == (stage == 0)
+        if stage == 0:
+            span = slice(None) if part is None else pl.ds(part * (rows // 2), rows // 2)
+            if along_x:
+                return gath.at[at, z, span, c]
+            return gath.at[x, at, span, c]
+        span = slice(None) if part is None else pl.ds(part * (side // 2), side // 2)
+        if along_x:
+            return gath.at[at, span, :, c]
+        return gath.at[span, at, :, c]
+
     sends = []
-    stage2 = []
-    stage1 = [[], []]
-    for f in range(2):
-        c = halves[f]
-        for k in range(1, side):
-            index = (f * 2 + 0) * side + k
-            copy = pltpu.make_async_remote_copy(
-                src_ref=h_ref.at[:, c], dst_ref=gath.at[x, z, :, c],
-                send_sem=send_sem.at[index], recv_sem=recv_sem.at[index],
-                device_id={"wa": peer(f, k)}, device_id_type=MESH)
-            copy.start()
-            sends.append(copy)
-            stage1[f].append(copy)
-    for f in range(2):
-        c = halves[f]
-        locals_[f].wait()
-        for copy in stage1[f]:
+    for stage in range(2):
+        first, geometry = {}, {}
+        for f in range(2):
+            along_x = (f == 0) == (stage == 0)
+            axis = 0 if along_x else 1
+            pos = x if along_x else z
+            base = (f * 2 + stage) * 4
+            geometry[f] = (axis, pos, base)
+            if stage == 0:
+                locals_[f].wait()
+            own = piece(f, stage, pos)
+            first[f] = []
+            for j, delta in enumerate((1, -1)):
+                copy = pltpu.make_async_remote_copy(
+                    src_ref=own, dst_ref=own,
+                    send_sem=send_sem.at[base + j], recv_sem=recv_sem.at[base + j],
+                    device_id={"wa": peer(axis, delta)}, device_id_type=MESH)
+                copy.start()
+                first[f].append(copy)
+                sends.append(copy)
+        second = []
+        for f in range(2):
+            axis, pos, base = geometry[f]
+            for j, delta in enumerate((1, -1)):
+                first[f][j].wait_recv()
+                origin = lax.rem(pos - delta + side, side)
+                part = piece(f, stage, origin, j)
+                copy = pltpu.make_async_remote_copy(
+                    src_ref=part, dst_ref=part,
+                    send_sem=send_sem.at[base + 2 + j], recv_sem=recv_sem.at[base + 2 + j],
+                    device_id={"wa": peer(axis, delta)}, device_id_type=MESH)
+                copy.start()
+                second.append(copy)
+                sends.append(copy)
+        for copy in second:
             copy.wait_recv()
-        if f == 0:
-            view = gath.at[:, z, :, c]
-        else:
-            view = gath.at[x, :, :, c]
-        for k in range(1, side):
-            index = (f * 2 + 1) * side + k
-            copy = pltpu.make_async_remote_copy(
-                src_ref=view, dst_ref=view,
-                send_sem=send_sem.at[index], recv_sem=recv_sem.at[index],
-                device_id={"wa": peer(1 - f, k)}, device_id_type=MESH)
-            copy.start()
-            stage2.append(copy)
     for copy in sends:
         copy.wait_send()
-    for copy in stage2:
-        copy.wait()
     final = pltpu.make_async_copy(gath, out_ref, local_sem.at[2])
     final.start()
     final.wait()

time: 178 us -> 177 us (level)
    pallas_call x1, Pallas kernels: 31.2 us -> 27 us  [grid_all_gather(): pl.pallas_call(functools.partial(_grid_ag_kernel, side, cols), out_shape=...]
    pallas_call x1, Pallas kernels: 20.8 us -> 23.7 us  [down_reduce_scatter(): pl.pallas_call(functools.partial(_down_rs_kernel, n, rows), out_shape=jax...]
where the time goes in v10:
time: 177 us
  Pallas kernels  168 us (95%)
  other arithmetic  6 us (3%)
  local copies, waits for them, and re-layouts  2.73 us (2%)
    pallas_call x1, Pallas kernels, ring_reduce_scatter(): pl.pallas_call(functools.partial(_ring_rs_kernel, side, cols, 2), out_sha...  85.5 us
    pallas_call x2, Pallas kernels, exchange(): pl.pallas_call(functools.partial(_exchange_kernel, mode, axis, n, rows),...  31.6 us
    pallas_call x1, Pallas kernels, grid_all_gather(): pl.pallas_call(functools.partial(_grid_ag_kernel, side, cols), out_shape=...  27 us
    pallas_call x1, Pallas kernels, down_reduce_scatter(): pl.pallas_call(functools.partial(_down_rs_kernel, n, rows), out_shape=jax...  23.7 us

profile of v10, /device:TPU:1, one launch (start us, length us, event | category | flops | bytes accessed | tf_op | source)
XLA Modules:
  0.0 176.6 jit_solution(8517834394877766989)
XLA Ops:
  0.0 1.0 fusion
  1.0 0.1 reshape.27
  1.1 0.6 pad.4.x_ref
  1.7 11.7 %shard_map.55 = f32[8,128]{1,0:T(8,128)} custom-call(f32[8,128]{1,0:T(8,128)} %pad.4.x_ref), custom_call_target="tpu_custom_call" | custom-call | tf_op jit(solution)/shard_map/pallas_call | solution.py:76
  13.4 0.7 add_rsqrt_fusion
  14.1 0.1 rsqrt.12
  14.2 1.7 fusion.2.x_ref
  15.9 19.9 %shard_map.56 = bf16[512,1024]{1,0:T(8,128)(2,1)} custom-call(bf16[64,1024]{1,0:T(8,128)(2,1)} %fusion.2.x_ref), custom_call_target="tpu_custom_call" | custom-call | tf_op jit(solution)/shard_map/pallas_call | solution.py:76
  35.8 85.5 %shard_map.57 = f32[32,6656]{1,0:T(8,128)} custom-call(bf16[4,4,32,1024]{3,2,1,0:T(8,128)(2,1)} %bitcast.3, bf16[1024,3328]{1,0:T(8,128)(2,1)} %g_hbm.1, bf16[1024,3328]{1,0:T(8,128)(2,1)} %u_hbm.1), custom_call_target="tpu_custom_call" | custom-call | tf_op jit(solution)/shard_map/pallas_call | solution.py:193
  121.3 1.9 %multiply_convert_fusion.h_ref = bf16[32,3328]{1,0:T(8,128)(2,1)} fusion(f32[32,6656]{1,0:T(8,128)} %shard_map.57), kind=kLoop, calls=%fused_computation | loop fusion | flops 638976 | bytes 1064960 | tf_op jit(solution)/shard_map/convert_element_type | solution.py:380
  123.2 27.0 %shard_map.58 = bf16[4,4,32,3328]{3,2,1,0:T(8,128)(2,1)} custom-call(bf16[32,3328]{1,0:T(8,128)(2,1)} %multiply_convert_fusion.h_ref), custom_call_target="tpu_custom_call" | custom-call | tf_op jit(solution)/shard_map/pallas_call | solution.py:302
  150.3 0.0 copy-start
  150.3 2.0 %copy-done = bf16[4,4,32,3328]{3,2,1,0:T(8,128)(2,1)S(1)} copy-done((bf16[4,4,32,3328]{3,2,1,0:T(8,128)(2,1)S(1)}, bf16[4,4,32,3328]{3,2,1,0:T(8,128)(2,1)}, u32[]{:S(2)}) %copy-start) | copy-done | bytes 3407896
  152.2 23.7 %shard_map.59 = f32[64,1024]{1,0:T(8,128)S(1)} custom-call(bf16[512,3328]{1,0:T(8,128)(2,1)S(1)} %bitcast.2, bf16[3328,1024]{1,0:T(8,128)(2,1)} %w_hbm.1), custom_call_target="tpu_custom_call" | custom-call | tf_op jit(solution)/shard_map/pallas_call | solution.py:346
  175.9 0.7 convert_element_type.17
Async XLA Ops:
  150.3 2.0 %copy-start = (bf16[4,4,32,3328]{3,2,1,0:T(8,128)(2,1)S(1)}, bf16[4,4,32,3328]{3,2,1,0:T(8,128)(2,1)}, u32[]{:S(2)}) copy-start(bf16[4,4,32,3328]{3,2,1,0:T(8,128)(2,1)} %shard_map.58) | copy-start | bytes 10223620

commit v11 on v10

--- a/solution.py
+++ b/solution.py
@@ -87,8 +87,8 @@
     )(x)
 
 
-def _ring_rs_kernel(side, cols, parts, t_ref, g_hbm, u_hbm, out_ref, wbuf, first_buf, tmp, recv1, acc1, s1,
-                    recv2, acc2, send_sem, recv_sem, w_sem):
+def _ring_rs_kernel(side, cols, parts, t_ref, g_hbm, u_hbm, out_ref, wbuf, first_buf, recv_b, tmp, recv1,
+                    acc1, s1, recv2, acc2, send_sem, recv_sem, w_sem):
     w = lax.axis_index("wa")
     x, z = w // side, lax.rem(w, side)
     loads = []
@@ -149,14 +149,18 @@
             chunk = lax.rem(pos1[f] - delta * (step + 1) + 2 * side, side)
             if step == 0:
                 loads[f].wait()
-                first_buf[f] = own1(f, chunk)
+                first_buf[f] = own1(f, chunk).astype(first_buf.dtype)
                 for h, r in enumerate(halves):
-                    send(0, step, f, h, first_buf.at[f, :, r], recv1.at[f, step, :, r], first)
+                    send(0, step, f, h, first_buf.at[f, :, r], recv_b.at[f, :, r], first)
             else:
                 tmp[f] = own1(f, chunk)
                 for h, r in enumerate(halves):
                     last[f][h].wait_recv()
-                    acc1[f, step - 1, :, r] = recv1[f, step - 1, :, r] + tmp[f, :, r]
+                    if step == 1:
+                        arrived = recv_b[f, :, r].astype(jnp.float32)
+                    else:
+                        arrived = recv1[f, step - 1, :, r]
+                    acc1[f, step - 1, :, r] = arrived + tmp[f, :, r]
                     send(0, step, f, h, acc1.at[f, step - 1, :, r], recv1.at[f, step, :, r], first)
     for f in range(4):
         first, delta, _ = flows[f]
@@ -198,7 +202,8 @@
         out_specs=pl.BlockSpec(memory_space=pltpu.VMEM),
         scratch_shapes=[
             pltpu.VMEM((4, depth, cols), gate_weight.dtype),
-            pltpu.VMEM((4, side, rows, cols), f32),
+            pltpu.VMEM((4, side, rows, cols), jnp.bfloat16),
+            pltpu.VMEM((4, side, rows, cols), jnp.bfloat16),
             pltpu.VMEM((4, side, rows, cols), f32),
             pltpu.VMEM((4, side - 1, side, rows, cols), f32),
             pltpu.VMEM((4, side - 2, side, rows, cols), f32),

time: 177 us -> 168 us (0.949)
  Pallas kernels: 168 us -> 159 us
    pallas_call x1, Pallas kernels: 85.5 us -> 76.4 us  [ring_reduce_scatter(): pl.pallas_call(functools.partial(_ring_rs_kernel, side, cols, 2), out_sha...]
where the time goes in v11:
time: 168 us; the launch traced here: 167 us
  Pallas kernels  159 us (95%)
  other arithmetic  6 us (4%)
  local copies, waits for them, and re-layouts  2.73 us (2%)
    pallas_call x1, Pallas kernels, ring_reduce_scatter(): pl.pallas_call(functools.partial(_ring_rs_kernel, side, cols, 2), out_sha...  76.4 us
    pallas_call x2, Pallas kernels, exchange(): pl.pallas_call(functools.partial(_exchange_kernel, mode, axis, n, rows),...  31.6 us
    pallas_call x1, Pallas kernels, grid_all_gather(): pl.pallas_call(functools.partial(_grid_ag_kernel, side, cols), out_shape=...  27 us
    pallas_call x1, Pallas kernels, down_reduce_scatter(): pl.pallas_call(functools.partial(_down_rs_kernel, n, rows), out_shape=jax...  23.7 us

profile of v11, /device:TPU:1, one launch (start us, length us, event | category | flops | bytes accessed | tf_op | source)
XLA Modules:
  0.0 167.5 jit_solution(12193577838195600002)
XLA Ops:
  0.0 1.0 fusion
  1.0 0.1 reshape.27
  1.1 0.6 pad.4.x_ref
  1.7 11.7 %shard_map.55 = f32[8,128]{1,0:T(8,128)} custom-call(f32[8,128]{1,0:T(8,128)} %pad.4.x_ref), custom_call_target="tpu_custom_call" | custom-call | tf_op jit(solution)/shard_map/pallas_call | solution.py:76
  13.4 0.7 add_rsqrt_fusion
  14.1 0.1 rsqrt.12
  14.2 1.7 fusion.2.x_ref
  15.9 19.9 %shard_map.56 = bf16[512,1024]{1,0:T(8,128)(2,1)} custom-call(bf16[64,1024]{1,0:T(8,128)(2,1)} %fusion.2.x_ref), custom_call_target="tpu_custom_call" | custom-call | tf_op jit(solution)/shard_map/pallas_call | solution.py:76
  35.8 76.4 %shard_map.57 = f32[32,6656]{1,0:T(8,128)} custom-call(bf16[4,4,32,1024]{3,2,1,0:T(8,128)(2,1)} %bitcast.3, bf16[1024,3328]{1,0:T(8,128)(2,1)} %g_hbm.1, bf16[1024,3328]{1,0:T(8,128)(2,1)} %u_hbm.1), custom_call_target="tpu_custom_call" | custom-call | tf_op jit(solution)/shard_map/pallas_call | solution.py:197
  112.2 1.9 %multiply_convert_fusion.h_ref = bf16[32,3328]{1,0:T(8,128)(2,1)} fusion(f32[32,6656]{1,0:T(8,128)} %shard_map.57), kind=kLoop, calls=%fused_computation | loop fusion | flops 638976 | bytes 1064960 | tf_op jit(solution)/shard_map/convert_element_type | solution.py:385
  114.1 27.0 %shard_map.58 = bf16[4,4,32,3328]{3,2,1,0:T(8,128)(2,1)} custom-call(bf16[32,3328]{1,0:T(8,128)(2,1)} %multiply_convert_fusion.h_ref), custom_call_target="tpu_custom_call" | custom-call | tf_op jit(solution)/shard_map/pallas_call | solution.py:307
  141.1 0.0 copy-start
  141.1 2.0 %copy-done = bf16[4,4,32,3328]{3,2,1,0:T(8,128)(2,1)S(1)} copy-done((bf16[4,4,32,3328]{3,2,1,0:T(8,128)(2,1)S(1)}, bf16[4,4,32,3328]{3,2,1,0:T(8,128)(2,1)}, u32[]{:S(2)}) %copy-start) | copy-done | bytes 3407896
  143.1 23.7 %shard_map.59 = f32[64,1024]{1,0:T(8,128)S(1)} custom-call(bf16[512,3328]{1,0:T(8,128)(2,1)S(1)} %bitcast.2, bf16[3328,1024]{1,0:T(8,128)(2,1)} %w_hbm.1), custom_call_target="tpu_custom_call" | custom-call | tf_op jit(solution)/shard_map/pallas_call | solution.py:351
  166.8 0.7 convert_element_type.17
Async XLA Ops:
  141.1 2.0 %copy-start = (bf16[4,4,32,3328]{3,2,1,0:T(8,128)(2,1)S(1)}, bf16[4,4,32,3328]{3,2,1,0:T(8,128)(2,1)}, u32[]{:S(2)}) copy-start(bf16[4,4,32,3328]{3,2,1,0:T(8,128)(2,1)} %shard_map.58) | copy-start | bytes 10223620

commit v12 on v11

--- a/solution.py
+++ b/solution.py
@@ -87,7 +87,7 @@
     )(x)
 
 
-def _ring_rs_kernel(side, cols, parts, t_ref, g_hbm, u_hbm, out_ref, wbuf, first_buf, recv_b, tmp, recv1,
+def _ring_rs_kernel(side, cols, parts, t_ref, g_hbm, u_hbm, out_ref, summed, wbuf, first_buf, recv_b, tmp, recv1,
                     acc1, s1, recv2, acc2, send_sem, recv_sem, w_sem):
     w = lax.axis_index("wa")
     x, z = w // side, lax.rem(w, side)
@@ -181,7 +181,10 @@
     for f in range(4):
         for h, r in enumerate(halves):
             last[f][h].wait_recv()
-            out_ref[r, flows[f][2]] = recv2[f, side - 2, r] + s1[f, pos2[f], r]
+            summed[r, flows[f][2]] = recv2[f, side - 2, r] + s1[f, pos2[f], r]
+    gate = summed[:, pl.ds(0, 2 * cols)]
+    up = summed[:, pl.ds(2 * cols, 2 * cols)]
+    out_ref[...] = (gate / (1.0 + jnp.exp(-gate)) * up).astype(out_ref.dtype)
     for copy in sends:
         copy.wait_send()
 
@@ -196,11 +199,12 @@
     f32 = jnp.float32
     return pl.pallas_call(
         functools.partial(_ring_rs_kernel, side, cols, 2),
-        out_shape=jax.ShapeDtypeStruct((rows, width), f32),
+        out_shape=jax.ShapeDtypeStruct((rows, width // 2), jnp.bfloat16),
         in_specs=[pl.BlockSpec(memory_space=pltpu.VMEM), pl.BlockSpec(memory_space=pl.ANY),
                   pl.BlockSpec(memory_space=pl.ANY)],
         out_specs=pl.BlockSpec(memory_space=pltpu.VMEM),
         scratch_shapes=[
+            pltpu.VMEM((rows, width), f32),
             pltpu.VMEM((4, depth, cols), gate_weight.dtype),
             pltpu.VMEM((4, side, rows, cols), jnp.bfloat16),
             pltpu.VMEM((4, side, rows, cols), jnp.bfloat16),
@@ -379,10 +383,7 @@
     normed = (own_values * lax.rsqrt(mean_square + 1e-05) * norm_gain[None, :]).astype(jnp.bfloat16)
     gathered = exchange(normed, "gather", "ha", n_ha, 1)
     hidden_width = gate_weight.shape[1]
-    summed = ring_reduce_scatter(gathered, gate_weight, up_weight, n_wa, 2)
-    gate = summed[:, :hidden_width]
-    up = summed[:, hidden_width:]
-    hidden = (jax.nn.silu(gate) * up).astype(jnp.bfloat16)
+    hidden = ring_reduce_scatter(gathered, gate_weight, up_weight, n_wa, 2)
     all_hidden = grid_all_gather(hidden, n_wa, 3)
     mixed_out = down_reduce_scatter(all_hidden, down_weight, n_ha, 4)
     return mixed_out.astype(jnp.bfloat16)

time: 168 us -> 166 us (0.988)
  other arithmetic: 6 us -> 4.05 us
    convert_element_type x1 -> x0, other arithmetic: 1.95 us -> none  [body(): hidden = (jax.nn.silu(gate) * up).astype(jnp.bfloat16)]
where the time goes in v12:
time: 166 us; the launch traced here: 165 us
  Pallas kernels  159 us (96%)
  other arithmetic  4.05 us (2%)
  local copies, waits for them, and re-layouts  2.73 us (2%)
    pallas_call x1, Pallas kernels, ring_reduce_scatter(): pl.pallas_call(functools.partial(_ring_rs_kernel, side, cols, 2), out_sha...  76.3 us
    pallas_call x2, Pallas kernels, exchange(): pl.pallas_call(functools.partial(_exchange_kernel, mode, axis, n, rows),...  31.6 us
    pallas_call x1, Pallas kernels, grid_all_gather(): pl.pallas_call(functools.partial(_grid_ag_kernel, side, cols), out_shape=...  27.1 us
    pallas_call x1, Pallas kernels, down_reduce_scatter(): pl.pallas_call(functools.partial(_down_rs_kernel, n, rows), out_shape=jax...  23.7 us

profile of v12, /device:TPU:1, one launch (start us, length us, event | category | flops | bytes accessed | tf_op | source)
XLA Modules:
  0.0 165.5 jit_solution(10395943206051848104)
XLA Ops:
  0.0 1.0 fusion
  1.0 0.1 reshape.27
  1.1 0.6 pad.4.x_ref
  1.7 11.7 %shard_map.55 = f32[8,128]{1,0:T(8,128)} custom-call(f32[8,128]{1,0:T(8,128)} %pad.4.x_ref), custom_call_target="tpu_custom_call" | custom-call | tf_op jit(solution)/shard_map/pallas_call | solution.py:76
  13.4 0.7 add_rsqrt_fusion
  14.1 0.1 rsqrt.12
  14.2 1.7 %fusion.2.x_ref = bf16[64,1024]{1,0:T(8,128)(2,1)} fusion(bf16[64,1024]{1,0:T(8,128)(2,1)} %param.5, f32[1024]{0:T(1024)} %param.6, f32[64]{0:T(128)S(1)} %rsqrt.12), kind=kLoop, calls=%fused_computation.4 | loop fusion | flops 262144 | bytes 266496 | tf_op jit(solution)/shard_map/convert_element_type | solution.py:383
  15.9 19.9 %shard_map.56 = bf16[512,1024]{1,0:T(8,128)(2,1)} custom-call(bf16[64,1024]{1,0:T(8,128)(2,1)} %fusion.2.x_ref), custom_call_target="tpu_custom_call" | custom-call | tf_op jit(solution)/shard_map/pallas_call | solution.py:76
  35.8 76.3 %shard_map.57.h_ref = bf16[32,3328]{1,0:T(8,128)(2,1)} custom-call(bf16[4,4,32,1024]{3,2,1,0:T(8,128)(2,1)} %bitcast.3, bf16[1024,3328]{1,0:T(8,128)(2,1)} %g_hbm.1, bf16[1024,3328]{1,0:T(8,128)(2,1)} %u_hbm.1), custom_call_target="tpu_custom_call" | custom-call | tf_op jit(solution)/shard_map/pallas_call | solution.py:200
  112.0 27.1 %shard_map.58 = bf16[4,4,32,3328]{3,2,1,0:T(8,128)(2,1)} custom-call(bf16[32,3328]{1,0:T(8,128)(2,1)} %shard_map.57.h_ref), custom_call_target="tpu_custom_call" | custom-call | tf_op jit(solution)/shard_map/pallas_call | solution.py:311
  139.1 0.0 copy-start
  139.1 2.0 %copy-done = bf16[4,4,32,3328]{3,2,1,0:T(8,128)(2,1)S(1)} copy-done((bf16[4,4,32,3328]{3,2,1,0:T(8,128)(2,1)S(1)}, bf16[4,4,32,3328]{3,2,1,0:T(8,128)(2,1)}, u32[]{:S(2)}) %copy-start) | copy-done | bytes 3407896
  141.1 23.7 %shard_map.59 = f32[64,1024]{1,0:T(8,128)S(1)} custom-call(bf16[512,3328]{1,0:T(8,128)(2,1)S(1)} %bitcast.2, bf16[3328,1024]{1,0:T(8,128)(2,1)} %w_hbm.1), custom_call_target="tpu_custom_call" | custom-call | tf_op jit(solution)/shard_map/pallas_call | solution.py:355
  164.8 0.7 convert_element_type.13
Async XLA Ops:
  139.1 2.0 %copy-start = (bf16[4,4,32,3328]{3,2,1,0:T(8,128)(2,1)S(1)}, bf16[4,4,32,3328]{3,2,1,0:T(8,128)(2,1)}, u32[]{:S(2)}) copy-start(bf16[4,4,32,3328]{3,2,1,0:T(8,128)(2,1)} %shard_map.58) | copy-start | bytes 10223620

commit v13 on v12

--- a/solution.py
+++ b/solution.py
@@ -331,7 +331,8 @@
     _greet("ha", n, me)
     load.wait()
     copies = []
-    for k in range(1, n):
+    order = sorted(range(1, n), key=lambda k: -min(k, n - k))
+    for k in order:
         peer = lax.rem(me + k, n)
         block = h_ref[pl.ds(pl.multiple_of(peer * rows, rows), rows), :]
         sendbuf[k] = jnp.dot(block, wbuf[...], preferred_element_type=jnp.float32).astype(sendbuf.dtype)
@@ -343,7 +344,7 @@
         copies.append(copy)
     block = h_ref[pl.ds(pl.multiple_of(me * rows, rows), rows), :]
     total = jnp.dot(block, wbuf[...], preferred_element_type=jnp.float32)
-    for k, copy in enumerate(copies, 1):
+    for k, copy in zip(order, copies):
         copy.wait()
         total = total + slots[k].astype(jnp.float32)
     out_ref[...] = total

time: 166 us -> 164 us (0.988)
  Pallas kernels: 159 us -> 156 us
    pallas_call x1, Pallas kernels: 23.7 us -> 21.4 us  [down_reduce_scatter(): pl.pallas_call(functools.partial(_down_rs_kernel, n, rows), out_shape=jax...]
where the time goes in v13:
time: 164 us; the launch traced here: 163 us
  Pallas kernels  156 us (95%)
  other arithmetic  4.05 us (2%)
  local copies, waits for them, and re-layouts  2.73 us (2%)
    pallas_call x1, Pallas kernels, ring_reduce_scatter(): pl.pallas_call(functools.partial(_ring_rs_kernel, side, cols, 2), out_sha...  76.3 us
    pallas_call x2, Pallas kernels, exchange(): pl.pallas_call(functools.partial(_exchange_kernel, mode, axis, n, rows),...  31.6 us
    pallas_call x1, Pallas kernels, grid_all_gather(): pl.pallas_call(functools.partial(_grid_ag_kernel, side, cols), out_shape=...  27.1 us
    pallas_call x1, Pallas kernels, down_reduce_scatter(): pl.pallas_call(functools.partial(_down_rs_kernel, n, rows), out_shape=jax...  21.4 us

profile of v13, /device:TPU:1, one launch (start us, length us, event | category | flops | bytes accessed | tf_op | source)
XLA Modules:
  0.0 163.2 jit_solution(8243039772369144664)
XLA Ops:
  0.0 1.0 fusion
  1.0 0.1 reshape.27
  1.1 0.6 pad.4.x_ref
  1.7 11.7 %shard_map.55 = f32[8,128]{1,0:T(8,128)} custom-call(f32[8,128]{1,0:T(8,128)} %pad.4.x_ref), custom_call_target="tpu_custom_call" | custom-call | tf_op jit(solution)/shard_map/pallas_call | solution.py:76
  13.4 0.7 add_rsqrt_fusion
  14.1 0.1 rsqrt.12
  14.2 1.7 %fusion.2.x_ref = bf16[64,1024]{1,0:T(8,128)(2,1)} fusion(bf16[64,1024]{1,0:T(8,128)(2,1)} %param.5, f32[1024]{0:T(1024)} %param.6, f32[64]{0:T(128)S(1)} %rsqrt.12), kind=kLoop, calls=%fused_computation.4 | loop fusion | flops 262144 | bytes 266496 | tf_op jit(solution)/shard_map/convert_element_type | solution.py:384
  15.9 19.9 %shard_map.56 = bf16[512,1024]{1,0:T(8,128)(2,1)} custom-call(bf16[64,1024]{1,0:T(8,128)(2,1)} %fusion.2.x_ref), custom_call_target="tpu_custom_call" | custom-call | tf_op jit(solution)/shard_map/pallas_call | solution.py:76
  35.8 76.3 %shard_map.57.h_ref = bf16[32,3328]{1,0:T(8,128)(2,1)} custom-call(bf16[4,4,32,1024]{3,2,1,0:T(8,128)(2,1)} %bitcast.3, bf16[1024,3328]{1,0:T(8,128)(2,1)} %g_hbm.1, bf16[1024,3328]{1,0:T(8,128)(2,1)} %u_hbm.1), custom_call_target="tpu_custom_call" | custom-call | tf_op jit(solution)/shard_map/pallas_call | solution.py:200
  112.0 27.1 %shard_map.58 = bf16[4,4,32,3328]{3,2,1,0:T(8,128)(2,1)} custom-call(bf16[32,3328]{1,0:T(8,128)(2,1)} %shard_map.57.h_ref), custom_call_target="tpu_custom_call" | custom-call | tf_op jit(solution)/shard_map/pallas_call | solution.py:311
  139.1 0.0 copy-start
  139.1 2.0 %copy-done = bf16[4,4,32,3328]{3,2,1,0:T(8,128)(2,1)S(1)} copy-done((bf16[4,4,32,3328]{3,2,1,0:T(8,128)(2,1)S(1)}, bf16[4,4,32,3328]{3,2,1,0:T(8,128)(2,1)}, u32[]{:S(2)}) %copy-start) | copy-done | bytes 3407896
  141.1 21.4 %shard_map.59 = f32[64,1024]{1,0:T(8,128)S(1)} custom-call(bf16[512,3328]{1,0:T(8,128)(2,1)S(1)} %bitcast.2, bf16[3328,1024]{1,0:T(8,128)(2,1)} %w_hbm.1), custom_call_target="tpu_custom_call" | custom-call | tf_op jit(solution)/shard_map/pallas_call | solution.py:356
  162.5 0.7 convert_element_type.13
Async XLA Ops:
  139.1 2.0 %copy-start = (bf16[4,4,32,3328]{3,2,1,0:T(8,128)(2,1)S(1)}, bf16[4,4,32,3328]{3,2,1,0:T(8,128)(2,1)}, u32[]{:S(2)}) copy-start(bf16[4,4,32,3328]{3,2,1,0:T(8,128)(2,1)} %shard_map.58) | copy-start | bytes 10223620

commit v14 on v13

--- a/solution.py
+++ b/solution.py
@@ -371,6 +371,59 @@
     )(hidden, down_weight)
 
 
+def _grid_sum_kernel(side, x_ref, out_ref, total1, slots1, slots2, send_sem, recv_sem):
+    w = lax.axis_index("wa")
+    x, z = w // side, lax.rem(w, side)
+
+    def peer(axis, k):
+        if axis == 0:
+            return lax.rem(x + k, side) * side + z
+        return x * side + lax.rem(z + k, side)
+
+    barrier = pltpu.get_barrier_semaphore()
+    for axis in (0, 1):
+        for k in range(1, side):
+            pl.semaphore_signal(barrier, inc=1, device_id={"wa": peer(axis, k)}, device_id_type=MESH)
+    pl.semaphore_wait(barrier, 2 * (side - 1))
+    for axis, source, slots, pos in ((0, x_ref, slots1, x), (1, total1, slots2, z)):
+        copies = []
+        for k in range(1, side):
+            copy = pltpu.make_async_remote_copy(
+                src_ref=source, dst_ref=slots.at[k],
+                send_sem=send_sem.at[axis * side + k], recv_sem=recv_sem.at[axis * side + k],
+                device_id={"wa": peer(axis, k)}, device_id_type=MESH)
+            copy.start()
+            copies.append(copy)
+        for copy in copies:
+            copy.wait()
+        slots[0] = source[...]
+        total = jnp.zeros(x_ref.shape, jnp.float32)
+        for sender in range(side):
+            total = total + slots[lax.rem(pos + side - sender, side)]
+        if axis == 0:
+            total1[...] = total
+        else:
+            out_ref[...] = total
+
+
+def grid_sum(x, collective_id):
+    side = 4
+    return pl.pallas_call(
+        functools.partial(_grid_sum_kernel, side),
+        out_shape=jax.ShapeDtypeStruct(x.shape, jnp.float32),
+        in_specs=[pl.BlockSpec(memory_space=pltpu.VMEM)],
+        out_specs=pl.BlockSpec(memory_space=pltpu.VMEM),
+        scratch_shapes=[
+            pltpu.VMEM(x.shape, jnp.float32),
+            pltpu.VMEM((side,) + x.shape, jnp.float32),
+            pltpu.VMEM((side,) + x.shape, jnp.float32),
+            pltpu.SemaphoreType.DMA((2 * side,)),
+            pltpu.SemaphoreType.DMA((2 * side,)),
+        ],
+        compiler_params=pltpu.CompilerParams(collective_id=collective_id, has_side_effects=True),
+    )(x)
+
+
 def body(tokens, norm_gain, gate_weight, up_weight, down_weight):
     n_wa = lax.axis_size("wa")
     n_ha = lax.axis_size("ha")
@@ -379,7 +432,7 @@
     own_rows = own_values.shape[0]
     partial_squares = jnp.sum(own_values * own_values, axis=1)
     packed = jnp.pad(partial_squares.reshape(8, own_rows // 8), ((0, 0), (0, 128 - own_rows // 8)))
-    squares = exchange(packed, "sum", "wa", n_wa, 0)[:, : own_rows // 8].reshape(own_rows, 1)
+    squares = grid_sum(packed, 0)[:, : own_rows // 8].reshape(own_rows, 1)
     mean_square = squares / model_width
     normed = (own_values * lax.rsqrt(mean_square + 1e-05) * norm_gain[None, :]).astype(jnp.bfloat16)
     gathered = exchange(normed, "gather", "ha", n_ha, 1)

time: 164 us -> 164 us (level)
    pallas_call x0 -> x1, Pallas kernels: none -> 12 us  [grid_sum(): pl.pallas_call(functools.partial(_grid_sum_kernel, side), out_shape=jax.S...]
    pallas_call x2 -> x1, Pallas kernels: 31.6 us -> 20.8 us  [exchange(): pl.pallas_call(functools.partial(_exchange_kernel, mode, axis, n, rows),...]
where the time goes in v14:
time: 164 us
  Pallas kernels  157 us (96%)
  other arithmetic  4.05 us (2%)
  local copies, waits for them, and re-layouts  2.73 us (2%)
    pallas_call x1, Pallas kernels, ring_reduce_scatter(): pl.pallas_call(functools.partial(_ring_rs_kernel, side, cols, 2), out_sha...  76 us
    pallas_call x1, Pallas kernels, grid_all_gather(): pl.pallas_call(functools.partial(_grid_ag_kernel, side, cols), out_shape=...  26.4 us
    pallas_call x1, Pallas kernels, down_reduce_scatter(): pl.pallas_call(functools.partial(_down_rs_kernel, n, rows), out_shape=jax...  21.6 us
    pallas_call x1, Pallas kernels, exchange(): pl.pallas_call(functools.partial(_exchange_kernel, mode, axis, n, rows),...  20.8 us
    pallas_call x1, Pallas kernels, grid_sum(): pl.pallas_call(functools.partial(_grid_sum_kernel, side), out_shape=jax.S...  12 us

profile of v14, /device:TPU:1, one launch (start us, length us, event | category | flops | bytes accessed | tf_op | source)
XLA Modules:
  0.0 163.6 jit_solution(16644129035339358093)
XLA Ops:
  0.0 1.0 fusion
  1.0 0.1 reshape.27
  1.1 0.6 pad.4.x_ref
  1.7 12.0 %shard_map.55 = f32[8,128]{1,0:T(8,128)} custom-call(f32[8,128]{1,0:T(8,128)} %pad.4.x_ref), custom_call_target="tpu_custom_call" | custom-call | tf_op jit(solution)/shard_map/pallas_call | solution.py:411
  13.8 0.7 add_rsqrt_fusion
  14.5 0.1 rsqrt.12
  14.5 1.7 %fusion.2.x_ref = bf16[64,1024]{1,0:T(8,128)(2,1)} fusion(bf16[64,1024]{1,0:T(8,128)(2,1)} %param.5, f32[1024]{0:T(1024)} %param.6, f32[64]{0:T(128)S(1)} %rsqrt.12), kind=kLoop, calls=%fused_computation.4 | loop fusion | flops 262144 | bytes 266496 | tf_op jit(solution)/shard_map/convert_element_type | solution.py:437
  16.2 20.8 %shard_map.56 = bf16[512,1024]{1,0:T(8,128)(2,1)} custom-call(bf16[64,1024]{1,0:T(8,128)(2,1)} %fusion.2.x_ref), custom_call_target="tpu_custom_call" | custom-call | tf_op jit(solution)/shard_map/pallas_call | solution.py:76
  37.0 76.0 %shard_map.57.h_ref = bf16[32,3328]{1,0:T(8,128)(2,1)} custom-call(bf16[4,4,32,1024]{3,2,1,0:T(8,128)(2,1)} %bitcast.3, bf16[1024,3328]{1,0:T(8,128)(2,1)} %g_hbm.1, bf16[1024,3328]{1,0:T(8,128)(2,1)} %u_hbm.1), custom_call_target="tpu_custom_call" | custom-call | tf_op jit(solution)/shard_map/pallas_call | solution.py:200
  113.0 26.4 %shard_map.58 = bf16[4,4,32,3328]{3,2,1,0:T(8,128)(2,1)} custom-call(bf16[32,3328]{1,0:T(8,128)(2,1)} %shard_map.57.h_ref), custom_call_target="tpu_custom_call" | custom-call | tf_op jit(solution)/shard_map/pallas_call | solution.py:311
  139.4 0.0 copy-start
  139.4 2.0 %copy-done = bf16[4,4,32,3328]{3,2,1,0:T(8,128)(2,1)S(1)} copy-done((bf16[4,4,32,3328]{3,2,1,0:T(8,128)(2,1)S(1)}, bf16[4,4,32,3328]{3,2,1,0:T(8,128)(2,1)}, u32[]{:S(2)}) %copy-start) | copy-done | bytes 3407896
  141.4 21.6 %shard_map.59 = f32[64,1024]{1,0:T(8,128)S(1)} custom-call(bf16[512,3328]{1,0:T(8,128)(2,1)S(1)} %bitcast.2, bf16[3328,1024]{1,0:T(8,128)(2,1)} %w_hbm.1), custom_call_target="tpu_custom_call" | custom-call | tf_op jit(solution)/shard_map/pallas_call | solution.py:356
  163.0 0.7 convert_element_type.13
Async XLA Ops:
  139.4 2.0 %copy-start = (bf16[4,4,32,3328]{3,2,1,0:T(8,128)(2,1)S(1)}, bf16[4,4,32,3328]{3,2,1,0:T(8,128)(2,1)}, u32[]{:S(2)}) copy-start(bf16[4,4,32,3328]{3,2,1,0:T(8,128)(2,1)} %shard_map.58) | copy-start | bytes 10223620

commit v15 on v13

--- a/solution.py
+++ b/solution.py
@@ -223,7 +223,7 @@
     )(t4, gate_weight, up_weight)
 
 
-def _grid_ag_kernel(side, cols, h_ref, out_ref, gath, send_sem, recv_sem, local_sem):
+def _grid_ag_kernel(side, cols, h_ref, gath, send_sem, recv_sem, local_sem):
     w = lax.axis_index("wa")
     x, z = w // side, lax.rem(w, side)
 
@@ -299,9 +299,6 @@
             copy.wait_recv()
     for copy in sends:
         copy.wait_send()
-    final = pltpu.make_async_copy(gath, out_ref, local_sem.at[2])
-    final.start()
-    final.wait()
 
 
 def grid_all_gather(h, n, collective_id):
@@ -314,7 +311,6 @@
         in_specs=[pl.BlockSpec(memory_space=pltpu.VMEM)],
         out_specs=pl.BlockSpec(memory_space=pltpu.VMEM),
         scratch_shapes=[
-            pltpu.VMEM((side, side, rows, width), h.dtype),
             pltpu.SemaphoreType.DMA((4 * side,)),
             pltpu.SemaphoreType.DMA((4 * side,)),
             pltpu.SemaphoreType.DMA((3,)),

time: 164 us -> 164 us (level)
  no operation moved by 1% of the time
where the time goes in v15:
time: 164 us; the launch traced here: 163 us
  Pallas kernels  156 us (95%)
  other arithmetic  4.05 us (2%)
  local copies, waits for them, and re-layouts  2.73 us (2%)
    pallas_call x1, Pallas kernels, ring_reduce_scatter(): pl.pallas_call(functools.partial(_ring_rs_kernel, side, cols, 2), out_sha...  76.3 us
    pallas_call x2, Pallas kernels, exchange(): pl.pallas_call(functools.partial(_exchange_kernel, mode, axis, n, rows),...  31.6 us
    pallas_call x1, Pallas kernels, grid_all_gather(): pl.pallas_call(functools.partial(_grid_ag_kernel, side, cols), out_shape=...  26.8 us
    pallas_call x1, Pallas kernels, down_reduce_scatter(): pl.pallas_call(functools.partial(_down_rs_kernel, n, rows), out_shape=jax...  21.4 us

profile of v15, /device:TPU:1, one launch (start us, length us, event | category | flops | bytes accessed | tf_op | source)
XLA Modules:
  0.0 163.0 jit_solution(6633108628336598272)
XLA Ops:
  0.0 1.0 fusion
  1.0 0.1 reshape.27
  1.1 0.6 pad.4.x_ref
  1.7 11.7 %shard_map.55 = f32[8,128]{1,0:T(8,128)} custom-call(f32[8,128]{1,0:T(8,128)} %pad.4.x_ref), custom_call_target="tpu_custom_call" | custom-call | tf_op jit(solution)/shard_map/pallas_call | solution.py:76
  13.4 0.7 add_rsqrt_fusion
  14.1 0.1 rsqrt.12
  14.2 1.7 %fusion.2.x_ref = bf16[64,1024]{1,0:T(8,128)(2,1)} fusion(bf16[64,1024]{1,0:T(8,128)(2,1)} %param.5, f32[1024]{0:T(1024)} %param.6, f32[64]{0:T(128)S(1)} %rsqrt.12), kind=kLoop, calls=%fused_computation.4 | loop fusion | flops 262144 | bytes 266496 | tf_op jit(solution)/shard_map/convert_element_type | solution.py:380
  15.9 19.9 %shard_map.56 = bf16[512,1024]{1,0:T(8,128)(2,1)} custom-call(bf16[64,1024]{1,0:T(8,128)(2,1)} %fusion.2.x_ref), custom_call_target="tpu_custom_call" | custom-call | tf_op jit(solution)/shard_map/pallas_call | solution.py:76
  35.8 76.3 %shard_map.57.h_ref = bf16[32,3328]{1,0:T(8,128)(2,1)} custom-call(bf16[4,4,32,1024]{3,2,1,0:T(8,128)(2,1)} %bitcast.3, bf16[1024,3328]{1,0:T(8,128)(2,1)} %g_hbm.1, bf16[1024,3328]{1,0:T(8,128)(2,1)} %u_hbm.1), custom_call_target="tpu_custom_call" | custom-call | tf_op jit(solution)/shard_map/pallas_call | solution.py:200
  112.0 26.8 %shard_map.58 = bf16[4,4,32,3328]{3,2,1,0:T(8,128)(2,1)} custom-call(bf16[32,3328]{1,0:T(8,128)(2,1)} %shard_map.57.h_ref), custom_call_target="tpu_custom_call" | custom-call | tf_op jit(solution)/shard_map/pallas_call | solution.py:308
  138.9 0.0 copy-start
  138.9 2.0 %copy-done = bf16[4,4,32,3328]{3,2,1,0:T(8,128)(2,1)S(1)} copy-done((bf16[4,4,32,3328]{3,2,1,0:T(8,128)(2,1)S(1)}, bf16[4,4,32,3328]{3,2,1,0:T(8,128)(2,1)}, u32[]{:S(2)}) %copy-start) | copy-done | bytes 3407896
  140.8 21.4 %shard_map.59 = f32[64,1024]{1,0:T(8,128)S(1)} custom-call(bf16[512,3328]{1,0:T(8,128)(2,1)S(1)} %bitcast.2, bf16[3328,1024]{1,0:T(8,128)(2,1)} %w_hbm.1), custom_call_target="tpu_custom_call" | custom-call | tf_op jit(solution)/shard_map/pallas_call | solution.py:352
  162.3 0.7 convert_element_type.13
Async XLA Ops:
  138.9 2.0 %copy-start = (bf16[4,4,32,3328]{3,2,1,0:T(8,128)(2,1)S(1)}, bf16[4,4,32,3328]{3,2,1,0:T(8,128)(2,1)}, u32[]{:S(2)}) copy-start(bf16[4,4,32,3328]{3,2,1,0:T(8,128)(2,1)} %shard_map.58) | copy-start | bytes 10223620

commit v16 on v15

--- a/solution.py
+++ b/solution.py
@@ -29,9 +29,13 @@
             source = x_ref.at[pl.ds(pl.multiple_of(peer * rows, rows), rows)]
         else:
             source = x_ref
+        if mode == "gather":
+            target = out_ref.at[pl.ds(pl.multiple_of(me * rows, rows), rows)]
+        else:
+            target = slots.at[k]
         copy = pltpu.make_async_remote_copy(
             src_ref=source,
-            dst_ref=slots.at[k],
+            dst_ref=target,
             send_sem=send_sem.at[k],
             recv_sem=recv_sem.at[k],
             device_id={axis: peer},
@@ -41,10 +45,8 @@
         copies.append(copy)
     if mode == "gather":
         out_ref[pl.ds(pl.multiple_of(me * rows, rows), rows), :] = x_ref[...]
-        for k, copy in enumerate(copies, 1):
+        for copy in copies:
             copy.wait()
-            sender = lax.rem(me + n - k, n)
-            out_ref[pl.ds(pl.multiple_of(sender * rows, rows), rows), :] = slots[k]
     elif mode == "scatter":
         total = x_ref[pl.ds(pl.multiple_of(me * rows, rows), rows), :].astype(jnp.float32)
         for k, copy in enumerate(copies, 1):

time: 164 us -> 164 us (level)
  no operation moved by 1% of the time
where the time goes in v16:
time: 164 us; the launch traced here: 163 us
  Pallas kernels  156 us (95%)
  other arithmetic  4.05 us (2%)
  local copies, waits for them, and re-layouts  2.73 us (2%)
    pallas_call x1, Pallas kernels, ring_reduce_scatter(): pl.pallas_call(functools.partial(_ring_rs_kernel, side, cols, 2), out_sha...  76.3 us
    pallas_call x2, Pallas kernels, exchange(): pl.pallas_call(functools.partial(_exchange_kernel, mode, axis, n, rows),...  31.5 us
    pallas_call x1, Pallas kernels, grid_all_gather(): pl.pallas_call(functools.partial(_grid_ag_kernel, side, cols), out_shape=...  26.8 us
    pallas_call x1, Pallas kernels, down_reduce_scatter(): pl.pallas_call(functools.partial(_down_rs_kernel, n, rows), out_shape=jax...  21.4 us

profile of v16, /device:TPU:1, one launch (start us, length us, event | category | flops | bytes accessed | tf_op | source)
XLA Modules:
  0.0 162.9 jit_solution(15543165694995349261)
XLA Ops:
  0.0 1.0 fusion
  1.0 0.1 reshape.27
  1.1 0.6 pad.4.x_ref
  1.7 11.7 %shard_map.55 = f32[8,128]{1,0:T(8,128)} custom-call(f32[8,128]{1,0:T(8,128)} %pad.4.x_ref), custom_call_target="tpu_custom_call" | custom-call | tf_op jit(solution)/shard_map/pallas_call | solution.py:78
  13.4 0.7 add_rsqrt_fusion
  14.1 0.1 rsqrt.12
  14.2 1.7 %fusion.2.x_ref = bf16[64,1024]{1,0:T(8,128)(2,1)} fusion(bf16[64,1024]{1,0:T(8,128)(2,1)} %param.5, f32[1024]{0:T(1024)} %param.6, f32[64]{0:T(128)S(1)} %rsqrt.12), kind=kLoop, calls=%fused_computation.4 | loop fusion | flops 262144 | bytes 266496 | tf_op jit(solution)/shard_map/convert_element_type | solution.py:382
  15.9 19.8 %shard_map.56 = bf16[512,1024]{1,0:T(8,128)(2,1)} custom-call(bf16[64,1024]{1,0:T(8,128)(2,1)} %fusion.2.x_ref), custom_call_target="tpu_custom_call" | custom-call | tf_op jit(solution)/shard_map/pallas_call | solution.py:78
  35.7 76.3 %shard_map.57.h_ref = bf16[32,3328]{1,0:T(8,128)(2,1)} custom-call(bf16[4,4,32,1024]{3,2,1,0:T(8,128)(2,1)} %bitcast.3, bf16[1024,3328]{1,0:T(8,128)(2,1)} %g_hbm.1, bf16[1024,3328]{1,0:T(8,128)(2,1)} %u_hbm.1), custom_call_target="tpu_custom_call" | custom-call | tf_op jit(solution)/shard_map/pallas_call | solution.py:202
  112.0 26.8 %shard_map.58 = bf16[4,4,32,3328]{3,2,1,0:T(8,128)(2,1)} custom-call(bf16[32,3328]{1,0:T(8,128)(2,1)} %shard_map.57.h_ref), custom_call_target="tpu_custom_call" | custom-call | tf_op jit(solution)/shard_map/pallas_call | solution.py:310
  138.9 0.0 copy-start
  138.9 2.0 %copy-done = bf16[4,4,32,3328]{3,2,1,0:T(8,128)(2,1)S(1)} copy-done((bf16[4,4,32,3328]{3,2,1,0:T(8,128)(2,1)S(1)}, bf16[4,4,32,3328]{3,2,1,0:T(8,128)(2,1)}, u32[]{:S(2)}) %copy-start) | copy-done | bytes 3407896
  140.8 21.4 %shard_map.59 = f32[64,1024]{1,0:T(8,128)S(1)} custom-call(bf16[512,3328]{1,0:T(8,128)(2,1)S(1)} %bitcast.2, bf16[3328,1024]{1,0:T(8,128)(2,1)} %w_hbm.1), custom_call_target="tpu_custom_call" | custom-call | tf_op jit(solution)/shard_map/pallas_call | solution.py:354
  162.3 0.7 convert_element_type.13
Async XLA Ops:
  138.9 2.0 %copy-start = (bf16[4,4,32,3328]{3,2,1,0:T(8,128)(2,1)S(1)}, bf16[4,4,32,3328]{3,2,1,0:T(8,128)(2,1)}, u32[]{:S(2)}) copy-start(bf16[4,4,32,3328]{3,2,1,0:T(8,128)(2,1)} %shard_map.58) | copy-start | bytes 10223620
